TPU v7x, 128 devices: a whole 4x4x4 slice. The times are simulated.
128 devices in a mesh: blk: 32 (over z, y, core), vec: 4 (over x).
Axes of the slice: x: 4, y: 4, z: 4, core: 2. Of those that a mesh axis runs over, the one named last changes fastest.
Arguments:
- label_features: bfloat16 [65536, 768], P('blk'), may hold values from -600 to 600
- start_basis: float32 [65536, 256], P('blk', 'vec'), may hold values from -6 to 6
- pair_block: int32 [32, 32], P('blk'), may hold values from 0 to 3
- pair_live: int32 [32, 32], P('blk'), may hold values from 0 to 1, as said below
Outputs:
- final_basis: float32 [65536, 256], P('blk', 'vec')
Inputs may be any that keep to these rules, and one draw needn't show every extreme that they name: pair_live is symmetric with zeros on its diagonal; owners differ widely in how many partners they have.
All inputs are finite; a program needn't handle non-finite values.
Results may differ from a plain program's by a relative error of at most 0.005.
Values may be sent and summed in bfloat16 or wider, within the bound.
No kernel may reach another device: no remote copies, remote signals or barrier semaphores. Data moves between devices by JAX's collectives and lax.ppermute only.
A program may use at most 192 MiB of HBM per device.

v0:
```python
import functools

import jax
import jax.numpy as jnp
from jax import lax
from jax.experimental import pallas as pl
from jax.experimental.pallas import tpu as pltpu
from jax.sharding import PartitionSpec as P


BS = 512
ITERS = 2
SHARPNESS = 5.0
EPSILON = 1e-06
AXES = ("blk", "vec")
HI = lax.Precision.HIGHEST
f32 = jnp.float32
bf16 = jnp.bfloat16


def normalize(features):
    widened = features.astype(f32)
    inv_norm = lax.rsqrt(jnp.mean(widened * widened, axis=-1, keepdims=True) + EPSILON)
    return (widened * inv_norm).astype(bf16)


LOG2E = 1.4426950408889634


def affinity(scores_sum, width):
    bent = scores_sum * (SHARPNESS * LOG2E / width)
    shift = SHARPNESS * LOG2E
    return (jnp.exp2(bent - shift) - jnp.exp2(-shift - bent)).astype(bf16)


def nt(a, b, **kw):
    return lax.dot_general(a, b, (((1,), (1,)), ((), ())), preferred_element_type=f32, **kw)


def spread(src, pb_ref, out_ref, sem):
    slots = out_ref.shape[0]
    for c in range(slots):
        pltpu.make_async_copy(src.at[pb_ref[c]], out_ref.at[c], sem.at[c]).start()
    for c in range(slots):
        pltpu.make_async_copy(src.at[0], out_ref.at[c], sem.at[c]).wait()


def own_quarter_body(my_ref, x_ref, *refs):
    half_refs, (buf, sem) = refs[:2], refs[2:]
    blocks, quarter, _ = buf.shape
    half = quarter // 2
    for t in range(blocks):
        pltpu.make_async_copy(
            x_ref.at[pl.ds(t * BS + my_ref[0] * quarter, quarter)], buf.at[t], sem.at[t]
        ).start()
    for t in range(blocks):
        pltpu.make_async_copy(x_ref.at[pl.ds(0, quarter)], buf.at[t], sem.at[t]).wait()
        unit = normalize(buf[t])
        for h, out_ref in enumerate(half_refs):
            out_ref[t] = unit[h * half : (h + 1) * half]


def own_quarter(x, my, blocks, quarter):
    feat = x.shape[1]
    vmem = pl.BlockSpec(memory_space=pltpu.VMEM)
    return pl.pallas_call(
        own_quarter_body,
        out_shape=[jax.ShapeDtypeStruct((blocks, quarter // 2, feat), bf16)] * 2,
        in_specs=[pl.BlockSpec(memory_space=pltpu.SMEM), pl.BlockSpec(memory_space=pl.ANY)],
        out_specs=[vmem] * 2,
        scratch_shapes=[pltpu.VMEM((blocks, quarter, feat), bf16), pltpu.SemaphoreType.DMA((blocks,))],
        name="own_quarter",
    )(my, x)


def cut_body(my_ref, basis_ref, *out_refs):
    quarter = BS // len(out_refs)
    for d, out_ref in enumerate(out_refs):
        for t in range(basis_ref.shape[1] // BS):
            at = pl.multiple_of(t * BS + (my_ref[0] ^ d) * quarter, quarter)
            out_ref[:, t * quarter : (t + 1) * quarter] = basis_ref[:, pl.ds(at, quarter)].astype(bf16)


def cut_start(basis_t, my, nvec):
    narrow, rows = basis_t.shape
    vmem = pl.BlockSpec(memory_space=pltpu.VMEM)
    return pl.pallas_call(
        cut_body,
        out_shape=[jax.ShapeDtypeStruct((narrow, rows // nvec), bf16)] * nvec,
        in_specs=[pl.BlockSpec(memory_space=pltpu.SMEM), vmem],
        out_specs=[vmem] * nvec,
        name="cut_start",
    )(my, basis_t)


NOTE = 16


def send_body(my_ref, pb_ref, v0_ref, v1_ref, v2_ref, v3_ref, own_ref, *refs):
    pack_refs, turned = refs[:2], refs[2]
    blocks, quarter, _ = own_ref.shape
    narrow = v0_ref.shape[0]
    for d, vt_ref in enumerate((v0_ref, v1_ref, v2_ref, v3_ref)):
        turned[my_ref[0] ^ d] = vt_ref[...].astype(f32).T.astype(bf16).reshape(blocks, quarter, narrow)
    own_ref[...] = jnp.concatenate([turned[g] for g in range(4)], axis=2)
    half = quarter // 2
    for h, pack in enumerate(pack_refs):
        pack[:, :half] = own_ref[:, h * half : (h + 1) * half]
        pack[:, half:] = jnp.zeros((blocks, NOTE, pack.shape[2]), bf16)
        pack[0, half:, :128] = pb_ref[...].astype(bf16)


def send_start(vts, pb, my, blocks, quarter):
    width = vts[0].shape[0] * len(vts)
    vmem = pl.BlockSpec(memory_space=pltpu.VMEM)
    note = jnp.broadcast_to(jnp.pad(pb.astype(f32), (0, 128 - pb.shape[0])), (NOTE, 128))
    out = pl.pallas_call(
        send_body,
        out_shape=[jax.ShapeDtypeStruct((blocks, quarter, width), bf16)]
        + [jax.ShapeDtypeStruct((blocks, quarter // 2 + NOTE, width), bf16)] * 2,
        in_specs=[pl.BlockSpec(memory_space=pltpu.SMEM), vmem] + [vmem] * len(vts),
        out_specs=[vmem] * 3,
        scratch_shapes=[pltpu.VMEM((len(vts), blocks, quarter, width // len(vts)), bf16)],
        name="send_start",
    )(my, note, *vts)
    return out[0], out[1:]


SHIFT = {"z": 3, "y": 1}
LINES = (("z", "y"), ("y", "z"))
NEAR = 4
SIDE = 8
STEPS = (0, 1, 3, 2)
FORWARD = (0, 4, 5, 2, 3, 6, 7, 1)


def near_at(h, d):
    return 2 * STEPS.index(d) + h


def side_at(h, o):
    return 2 * FORWARD.index(o) + h


def offset(axis, o):
    return (o >> 1) << SHIFT[axis] | (o & 1)


def relay_body(at_ref, *refs):
    feat_refs, vec_refs = refs[: 2 * NEAR], refs[2 * NEAR : 4 * NEAR]
    out_refs, (notes, pbs, sem_note, sem) = refs[4 * NEAR : -4], refs[-4:]
    owner = at_ref[0]
    _, half, feat = feat_refs[0].shape
    width = vec_refs[0].shape[2]
    for i, vec in enumerate(vec_refs):
        notes[i : i + 1] = vec[0, half:, :128].astype(f32)[:1].astype(jnp.int32)
    note_copy = pltpu.make_async_copy(notes, pbs, sem_note)
    note_copy.start()
    note_copy.wait()

    def copies(h, o, d, block):
        out = out_refs[side_at(h, o)]
        i = near_at(h, d)
        return (
            pltpu.make_async_copy(feat_refs[i].at[block], out.at[d, :, pl.ds(0, feat)], sem.at[h, o]),
            pltpu.make_async_copy(
                vec_refs[i].at[block, pl.ds(0, half)], out.at[d, :, pl.ds(feat, width)], sem.at[h, o]
            ),
        )

    places = [(h, o, d) for o in FORWARD for h in range(2) for d in range(NEAR)]
    for h, o, d in places:
        for copy in copies(h, o, d, pbs[near_at(h, d), owner ^ offset(LINES[h][1], o)]):
            copy.start()
    for h in range(2):
        for o in range(SIDE):
            out = out_refs[side_at(h, o)]
            pltpu.make_async_copy(out, out, sem.at[h, o]).wait()


def relay(feats, vecs, owner):
    _, half, feat = feats[0].shape
    hbm = pl.BlockSpec(memory_space=pl.ANY)
    vmem = pl.BlockSpec(memory_space=pltpu.VMEM)
    shape = jax.ShapeDtypeStruct((NEAR, half, feat + vecs[0].shape[2]), bf16)
    return pl.pallas_call(
        relay_body,
        out_shape=[shape] * (2 * SIDE),
        in_specs=[pl.BlockSpec(memory_space=pltpu.SMEM)] + [vmem] * (len(feats) + len(vecs)),
        out_specs=[hbm] * (2 * SIDE),
        scratch_shapes=[
            pltpu.VMEM((2 * NEAR, 128), jnp.int32),
            pltpu.SMEM((2 * NEAR, 128), jnp.int32),
            pltpu.SemaphoreType.DMA(()),
            pltpu.SemaphoreType.DMA((2, SIDE)),
        ],
        name="relay",
    )(owner, *feats, *vecs)


LANES = 4
HALF = 2


def pair_table(pb, live, owner, blocks, entries):
    slots = pb.shape[0]
    on = live > 0
    c = jnp.arange(slots, dtype=jnp.int32)
    same = (pb[:, None] == pb[None, :]) & on[None, :] & (c[None, :] < c[:, None])
    rank = jnp.sum(same.astype(jnp.int32), axis=1)
    t = jnp.arange(blocks, dtype=jnp.int32)
    number = jnp.sum(((pb[None, :] == t[:, None]) & on[None, :]).astype(jnp.int32), axis=1)
    even = (number + 1) // 2 * 2
    plain = jnp.sum(jnp.where(t[None, :] <= t[:, None], even[None, :], 0), axis=1)
    middle = jnp.sum(jnp.where(t < HALF, even, 0))
    pad = -middle % LANES
    end = plain + jnp.where(t >= HALF - 1, pad, 0)
    begin = plain - even + jnp.where(t >= HALF, pad, 0)
    start = jnp.sum(jnp.where(pb[:, None] == t[None, :], begin[None, :], 0), axis=1)
    at = jnp.where(on, start + rank, -1)
    j = jnp.arange(entries, dtype=jnp.int32)
    hit = at[None, :] == j[:, None]
    slot = jnp.sum(jnp.where(hit, c[None, :], 0), axis=1)
    use = jnp.sum(hit.astype(jnp.int32), axis=1)
    target = jnp.minimum(jnp.sum((j[:, None] >= end[None, :]).astype(jnp.int32), axis=1), blocks - 1)
    by_offset = jnp.sum(jnp.where((owner ^ c)[:, None] == c[None, :], at[None, :], 0), axis=1)
    return jnp.concatenate([slot, use, target, end[-1:], by_offset, (middle + pad)[None]])


def entries_of(slots, blocks):
    return -(-(slots - 1 + blocks) // LANES) * LANES


def add_product(out_refs, t, p, first):
    quarter = out_refs[0].shape[1]
    for d, out_ref in enumerate(out_refs):
        piece = p[d * quarter : (d + 1) * quarter]
        if first:
            out_ref[t] = piece
        else:
            out_ref[t] += piece


def entry_range(sc, entries, slots, part):
    middle = sc[3 * entries + 1 + slots]
    return (0, middle) if part == 0 else (middle, sc[3 * entries])


def pairs_first_body(entries, part, sc_ref, my_ref, unit_ref, *refs):
    far_refs, refs = refs[: 2 * SIDE], refs[2 * SIDE :]
    vown_ref, aff_ref, out_refs, (buf, sem) = refs[0], refs[1], refs[2:-2], refs[-2:]
    quarter = vown_ref.shape[1]
    half = quarter // 2
    feat = unit_ref.shape[1]
    slots = NEAR * NEAR * 2
    s = pl.program_id(0)
    v = my_ref[0]
    low, high = entry_range(sc_ref, entries, slots, part)

    def copy(h, side, line, entry):
        return pltpu.make_async_copy(
            far_refs[side_at(h, side)].at[line], buf.at[entry, pl.ds(h * half, half)], sem.at[h, entry]
        )

    def target_rows(t):
        return jnp.concatenate(
            [unit_ref[pl.ds(t * BS + (v ^ d) * quarter, quarter), :] for d in range(len(out_refs))], axis=0
        )

    @pl.when(s == 0)
    def _():
        for o in range(1, slots):
            z, y, core = o >> 3, (o >> 1) & 3, o & 1
            entry = sc_ref[3 * entries + 1 + o]

            @pl.when((entry >= low) & (entry < high))
            def _():
                copy(0, 2 * y + core, z, entry).start()
                copy(1, 2 * z + core, y, entry).start()

        def own(t, _):
            rows = target_rows(t)
            aff = affinity(nt(rows, rows[:quarter]), feat)
            aff_ref[t] = aff
            p = jnp.dot(aff, vown_ref[part * HALF + t], preferred_element_type=f32)
            add_product(out_refs, t, p, True)
            return 0

        lax.fori_loop(0, HALF, own, 0)

    @pl.when((s > 0) & (low + (s - 1) * LANES < high))
    def _():
        first = jnp.clip(low + (s - 1) * LANES, 0, entries - LANES)

        def two(i, _):
            at = first + 2 * i
            used = [sc_ref[entries + at + k] > 0 for k in range(2)]
            for k in range(2):

                @pl.when(used[k])
                def _():
                    copy(0, 0, 0, at + k).wait()
                    copy(1, 0, 0, at + k).wait()

            t = jnp.clip(sc_ref[2 * entries + at] - part * HALF, 0, HALF - 1)
            rhs = jnp.concatenate([buf[at + k, :, :feat] for k in range(2)], axis=0)
            both = affinity(nt(target_rows(t), rhs), feat)
            affs, vecs = [], []
            for k in range(2):
                aff = both[:, k * quarter : (k + 1) * quarter]
                aff = jnp.where(used[k], aff, jnp.zeros_like(aff))
                vec = buf[at + k, :, feat:]
                vecs.append(jnp.where(used[k], vec, jnp.zeros_like(vec)))
                aff_ref[2 * i + k] = aff
                affs.append(aff)
            p = jnp.dot(
                jnp.concatenate(affs, axis=1), jnp.concatenate(vecs, axis=0), preferred_element_type=f32
            )
            add_product(out_refs, t, p, False)
            return 0

        lax.fori_loop(0, LANES // 2, two, 0)


def pairs_next_body(entries, part, sc_ref, my_ref, aff_ref, *refs):
    far_refs, vown_ref, out_refs = refs[:LANES], refs[LANES], refs[LANES + 1 :]
    s = pl.program_id(0)
    low, high = entry_range(sc_ref, entries, NEAR * NEAR * 2, part)

    @pl.when(s == 0)
    def _():
        def own(t, _):
            p = jnp.dot(aff_ref[t], vown_ref[part * HALF + t], preferred_element_type=f32)
            add_product(out_refs, t, p, True)
            return 0

        lax.fori_loop(0, HALF, own, 0)

    @pl.when((s > 0) & (low + (s - 1) * LANES < high))
    def _():
        first = jnp.clip(low + (s - 1) * LANES, 0, entries - LANES)
        for k in range(0, LANES, 2):
            t = jnp.clip(sc_ref[2 * entries + first + k] - part * HALF, 0, HALF - 1)
            aff = jnp.concatenate([aff_ref[k], aff_ref[k + 1]], axis=1)
            vec = jnp.concatenate([far_refs[k][0], far_refs[k + 1][0]], axis=0)
            add_product(out_refs, t, jnp.dot(aff, vec, preferred_element_type=f32), False)


def pair_specs(blocks, quarter, width, entries, part):
    quarters = BS // quarter
    whole = lambda s, sc, my: (0, 0, 0)

    def last_step(sc):
        low, high = entry_range(sc, entries, NEAR * NEAR * 2, part)
        return (high - low + LANES - 1) // LANES

    def slot_map(k):
        def index(s, sc, my):
            low, _ = entry_range(sc, entries, NEAR * NEAR * 2, part)
            first = low + jnp.maximum(jnp.minimum(s, last_step(sc)) - 1, 0) * LANES
            return (sc[jnp.minimum(first, entries - LANES) + k], 0, 0)

        return index

    aff_spec = pl.BlockSpec((LANES, BS, quarter), lambda s, sc, my: (jnp.minimum(s, last_step(sc)), 0, 0))
    own_spec = pl.BlockSpec((blocks, quarter, width), whole)
    out_spec = pl.BlockSpec((HALF, quarter, width), whole)
    out_shapes = [jax.ShapeDtypeStruct((HALF, quarter, width), f32)] * quarters
    far_specs = [pl.BlockSpec((1, quarter, width), slot_map(k)) for k in range(LANES)]
    return aff_spec, own_spec, far_specs, [out_spec] * quarters, out_shapes


def pairs_first(sc, my, unit, fars, vown, entries, part):
    blocks, quarter, width = vown.shape
    far_width = fars[0].shape[2]
    aff_spec, own_spec, _, out_specs, out_shapes = pair_specs(blocks, quarter, width, entries, part)
    out = pl.pallas_call(
        functools.partial(pairs_first_body, entries, part),
        out_shape=[jax.ShapeDtypeStruct((LANES + entries, BS, quarter), bf16)] + out_shapes,
        grid_spec=pltpu.PrefetchScalarGridSpec(
            num_scalar_prefetch=2,
            grid=(1 + entries // LANES,),
            in_specs=[pl.BlockSpec((HALF * BS, unit.shape[1]), lambda s, sc, my: (part, 0))]
            + [pl.BlockSpec(memory_space=pl.ANY)] * len(fars)
            + [own_spec],
            out_specs=[aff_spec] + out_specs,
            scratch_shapes=[
                pltpu.VMEM((entries, quarter, far_width), bf16),
                pltpu.SemaphoreType.DMA((2, entries)),
            ],
        ),
        cost_estimate=pl.CostEstimate(flops=6 * 10**9, bytes_accessed=12 * 2**20, transcendentals=2 * 10**6),
    )(sc, my, unit, *fars, vown)
    return out[0], out[1:]


def pairs_next(sc, my, far, vown, aff, entries, part):
    blocks, quarter, width = vown.shape
    aff_spec, own_spec, far_specs, out_specs, out_shapes = pair_specs(blocks, quarter, width, entries, part)
    return pl.pallas_call(
        functools.partial(pairs_next_body, entries, part),
        out_shape=out_shapes,
        grid_spec=pltpu.PrefetchScalarGridSpec(
            num_scalar_prefetch=2,
            grid=(1 + entries // LANES,),
            in_specs=[aff_spec] + far_specs + [own_spec],
            out_specs=out_specs,
        ),
        cost_estimate=pl.CostEstimate(flops=2 * 10**9, bytes_accessed=12 * 2**20, transcendentals=0),
    )(sc, my, aff, *[far] * LANES, vown)


def gram_body(nvec, my_ref, *refs):
    part_refs, prod_ref, piece_refs, full = refs[:nvec], refs[nvec], refs[nvec + 1 : -1], refs[-1]
    rows = part_refs[0].shape[0]
    for i in range(0, nvec, 4):
        a, b, c, d = (r[...] for r in part_refs[i : i + 4])
        prod_ref[(i // 4) * rows : (i // 4 + 1) * rows] = (a + b) + (c + d)
    p = prod_ref[...]
    full[...] = lax.dot_general(
        p, p, (((0,), (0,)), ((), ())), precision=HI, preferred_element_type=f32
    )
    for d, piece in enumerate(piece_refs):
        rows = piece.shape[0]
        piece[...] = full[pl.ds(pl.multiple_of((my_ref[0] ^ d) * rows, rows), rows), :]


def gram(parts, my, nvec):
    rows, width = parts[0].shape
    vmem = pl.BlockSpec(memory_space=pltpu.VMEM)
    out = pl.pallas_call(
        functools.partial(gram_body, len(parts)),
        out_shape=[jax.ShapeDtypeStruct((rows * len(parts) // nvec, width), f32)]
        + [jax.ShapeDtypeStruct((width // nvec, width), f32)] * nvec,
        in_specs=[pl.BlockSpec(memory_space=pltpu.SMEM)] + [vmem] * len(parts),
        out_specs=[vmem] * (nvec + 1),
        scratch_shapes=[pltpu.VMEM((width, width), f32)],
        name="gram",
    )(my, *parts)
    return out[0], out[1:]


def lane_splat(x, j):
    return jnp.broadcast_to(x[:, j : j + 1], x.shape)


def row_splat(x, s):
    return jnp.broadcast_to(x[s : s + 1, :], x.shape)


def split3(x):
    high = x.astype(bf16)
    rest = x - high.astype(f32)
    mid = rest.astype(bf16)
    return high, mid, (rest - mid.astype(f32)).astype(bf16)


PANEL = 16


def inverse_factor(a):
    n = a.shape[0]
    row_at = lax.broadcasted_iota(jnp.int32, (PANEL, n), 0)
    square = (n, n)
    on_diag = lax.broadcasted_iota(jnp.int32, square, 0) == lax.broadcasted_iota(jnp.int32, square, 1)
    inv = jnp.where(on_diag, 1.0, 0.0).astype(f32)
    done = []
    for j in range(0, n, PANEL):
        top, itop = a[:PANEL, :], inv[:PANEL, :]
        cols = [lane_splat(top, j + c) for c in range(PANEL)]
        for c in range(PANEL):
            scale = lax.rsqrt(row_splat(cols[c], c))
            below = jnp.where(row_at > c, cols[c] * scale, 0.0)
            for k in range(c + 1, PANEL):
                cols[k] = cols[k] - below * (row_splat(cols[k], c) * scale)
            row, irow = row_splat(top, c) * scale, row_splat(itop, c) * scale
            top = jnp.where(row_at == c, row, top - below * row)
            itop = jnp.where(row_at == c, irow, itop - below * irow)
        done.append(itop)
        if j + PANEL < n:
            h, m, l = split3(top)
            ih, im, il = split3(itop)
            left = jnp.concatenate([h, h, m, h, l, m], axis=0)
            right = jnp.concatenate(
                [jnp.concatenate([h, m, h, l, h, m], axis=0), jnp.concatenate([ih, im, ih, il, ih, im], axis=0)],
                axis=1,
            )
            update = lax.dot_general(left, right, (((0,), (0,)), ((), ())), preferred_element_type=f32)
            update = update[j + PANEL :, :]
            a = a[PANEL:, :] - update[:, :n]
            inv = inv[PANEL:, :] - update[:, n:]
    return jnp.concatenate(done, axis=0)


def whiten(my_ref, chunk_refs, a_ref, w_ref, label_total):
    n = a_ref.shape[0]
    h = n // 2
    rows = chunk_refs[0].shape[0]
    for d, chunk in enumerate(chunk_refs):
        at = pl.multiple_of((my_ref[0] ^ d) * rows, rows)
        a_ref[pl.ds(at, rows), :] = chunk[...] * (1.0 / label_total)

    def half(i, _):
        at = pl.multiple_of(i * h, h)
        w = inverse_factor(a_ref[pl.ds(at, h), :h])
        w_ref[pl.ds(at, h), h:] = w

        @pl.when(i == 0)
        def _():
            low = nt(a_ref[h:, :h], w, precision=HI)
            w_ref[:h, :h] = jnp.dot(low, w, precision=HI, preferred_element_type=f32)
            a_ref[h:, :h] = a_ref[h:, h:] - nt(low, low, precision=HI)

        return 0

    lax.fori_loop(0, 2, half, 0)
    w11, w22, mid = w_ref[:h, h:], w_ref[h:, h:], w_ref[:h, :h]
    w_ref[h:, :h] = -jnp.dot(w22, mid, precision=HI, preferred_element_type=f32)
    w_ref[:h, :h] = w11
    w_ref[:h, h:] = jnp.zeros((h, h), f32)


def step_body(label_total, chunks, my_ref, pb_ref, *refs):
    chunk_refs, (prod_ref, own_ref, out_ref, a_ref, w_ref, sem) = refs[:chunks], refs[chunks:]
    whiten(my_ref, chunk_refs, a_ref, w_ref, label_total)
    own_ref[...] = nt(prod_ref[...], w_ref[...], precision=HI).astype(bf16).reshape(own_ref.shape)
    spread(own_ref, pb_ref, out_ref, sem)


def step(gram_chunks, prod, my, pb, blocks, quarter, label_total):
    width = prod.shape[1]
    slots = pb.shape[0]
    chunks = len(gram_chunks)
    smem = pl.BlockSpec(memory_space=pltpu.SMEM)
    vmem = pl.BlockSpec(memory_space=pltpu.VMEM)
    return pl.pallas_call(
        functools.partial(step_body, label_total, chunks),
        out_shape=(
            jax.ShapeDtypeStruct((blocks, quarter, width), bf16),
            jax.ShapeDtypeStruct((slots, quarter, width), bf16),
        ),
        in_specs=[smem, smem] + [vmem] * (chunks + 1),
        out_specs=(vmem, pl.BlockSpec(memory_space=pl.ANY)),
        scratch_shapes=[
            pltpu.VMEM((width, width), f32),
            pltpu.VMEM((width, width), f32),
            pltpu.SemaphoreType.DMA((slots,)),
        ],
        name="step",
    )(my, pb, *gram_chunks, prod)


def last_body(label_total, chunks, my_ref, *refs):
    chunk_refs, prod_refs, (out_ref, a_ref, w_ref) = refs[:chunks], refs[chunks:-3], refs[-3:]
    whiten(my_ref, chunk_refs, a_ref, w_ref, label_total)
    narrow, rows = out_ref.shape
    quarter = BS // len(prod_refs)
    v = my_ref[0]
    w = w_ref[pl.ds(pl.multiple_of(v * narrow, narrow), narrow), :]
    for d, prod_ref in enumerate(prod_refs):
        piece = nt(w, prod_ref[...], precision=HI)
        for t in range(rows // BS):
            at = pl.multiple_of(t * BS + (v ^ d) * quarter, quarter)
            out_ref[:, pl.ds(at, quarter)] = piece[:, t * quarter : (t + 1) * quarter]


def last(gram_chunks, prods, my, label_total):
    rows, width = prods[0].shape
    chunks = len(gram_chunks)
    smem = pl.BlockSpec(memory_space=pltpu.SMEM)
    vmem = pl.BlockSpec(memory_space=pltpu.VMEM)
    return pl.pallas_call(
        functools.partial(last_body, label_total, chunks),
        out_shape=jax.ShapeDtypeStruct((width // len(prods), rows * len(prods)), f32),
        in_specs=[smem] + [vmem] * (chunks + len(prods)),
        out_specs=vmem,
        scratch_shapes=[pltpu.VMEM((width, width), f32), pltpu.VMEM((width, width), f32)],
        name="last",
    )(my, *gram_chunks, *prods)


def make(mesh):
    nblk, nvec = mesh.shape["blk"], mesh.shape["vec"]

    def swap(x, owner_bits, vec_bits):
        perm = [
            (o * nvec + v, (o ^ owner_bits) * nvec + (v ^ vec_bits))
            for o in range(nblk)
            for v in range(nvec)
        ]
        return lax.ppermute(x, AXES, perm)

    def exchange(x, axis):
        return lax.all_to_all(x, axis, split_axis=0, concat_axis=0, tiled=True)

    def gram_sum(pieces, prod, gather):
        total = pieces[0]
        for d in range(1, nvec):
            total = total + swap(pieces[d], 0, d)
        prods = [prod]
        if gather:
            total, prod = lax.optimization_barrier((total, prod))
            prods = [prod] + [swap(prod, 0, d) for d in range(1, nvec)]
        for shift in (1, 3):
            got = [swap(total, d << shift, 0) for d in (1, 2, 3)]
            total = (total + got[0]) + (got[1] + got[2])
        total = total + swap(total, 1, 0)
        return [total] + [swap(total, 0, d) for d in range(1, nvec)], prods

    def body(x, basis, pair_block, pair_live):
        rows, _ = x.shape
        narrow = basis.shape[1]
        blocks = rows // BS
        quarter = BS // nvec
        label_total = rows * nblk
        v = lax.axis_index("vec")
        my = v[None].astype(jnp.int32)
        pb, live = pair_block[0], pair_live[0]

        owner = lax.axis_index("blk").astype(jnp.int32)
        cuts = cut_start(basis.T, my, nvec)
        x, cuts = lax.optimization_barrier((x, cuts))
        vts = [cuts[0]] + [swap(cuts[d], 0, d) for d in range(1, nvec)]
        units = own_quarter(x, my, blocks, quarter)
        units, vts = lax.optimization_barrier((units, vts))

        def along(x, h, d):
            return x if d == 0 else swap(x, d << SHIFT[LINES[h][0]], 0)

        feats = [along(units[h], h, d) for d in STEPS for h in range(2)]
        vown, packs = send_start(vts, pb, my, blocks, quarter)
        vecs = [along(packs[h], h, d) for d in STEPS for h in range(2)]
        sends = relay(feats, vecs, owner[None])
        fars = [
            sends[side_at(h, o)] if o == 0 else swap(sends[side_at(h, o)], offset(LINES[h][1], o), 0)
            for o in FORWARD
            for h in range(2)
        ]

        (x, pb_late, live), fars[2] = lax.optimization_barrier(((x, pb, live), fars[2]))
        entries = entries_of(nblk, blocks)
        sc = pair_table(pb_late, live, owner, blocks, entries)
        unit = normalize(x)

        affs = [None] * (blocks // HALF)
        for it in range(ITERS):
            parts = []
            for part in range(len(affs)):
                if it:
                    out = pairs_next(sc, my, far, vown, affs[part], entries, part)
                else:
                    affs[part], out = pairs_first(sc, my, unit, fars, vown, entries, part)
                sc, out = lax.optimization_barrier((sc, list(out)))
                out = [o.reshape(HALF * quarter, nvec * narrow) for o in out]
                parts.append(out[0])
                for d in range(1, nvec):
                    parts.append(swap(out[d], 0, d))
            prod, pieces = gram(parts, my, nvec)
            sums, prods = gram_sum(pieces, prod, it + 1 == ITERS)
            if it + 1 < ITERS:
                vown, vsend = step(sums, prod, my, pb, blocks, quarter, label_total)
                far = exchange(vsend, "blk")
        return last(sums, prods, my, label_total).T

    return body


def solution(mesh):
    in_specs = (P("blk", None), P("blk", "vec"), P("blk", None), P("blk", None))
    return jax.shard_map(
        make(mesh), mesh=mesh, in_specs=in_specs, out_specs=P("blk", "vec"), check_vma=False
    )
```

profile of v0, /device:TPU:0, one launch (start us, length us, event | category | flops | bytes accessed | tf_op | source)
XLA Modules:
  0.0 364.2 jit_solution(8313146591104731482)
XLA Ops:
  3.6 2.7 collective-permute-start.1
  12.6 3.9 %collective-permute-start.7 = (bf16[4,64,768]{2,1,0:T(8,128)(2,1)}, bf16[4,64,768]{2,1,0:T(8,128)(2,1)S(1)}, u32[]{:S(2)}, u32[]{:S(2)}) collective-permute-start(bf16[4,64,768]{2,1,0:T(8,128)(2,1)} %get-tuple-element.107.refs_0_), channel_id=1, source_target_pairs={{0,64},{1,65},{2,66},{3,67},{4,68},{5,69},{6,70},{7,71},{8,72},{9,... | collective-permute-start | bytes 1179656 | tf_op jit(solution)/shard_map/ppermute | solution.py:591
  19.9 3.7 %collective-permute-start.11 = (bf16[4,80,256]{2,1,0:T(8,128)(2,1)}, bf16[4,80,256]{2,1,0:T(8,128)(2,1)S(1)}, u32[]{:S(2)}, u32[]{:S(2)}) collective-permute-start(bf16[4,80,256]{2,1,0:T(8,128)(2,1)} %get-tuple-element.113.refs_8_), channel_id=1, source_target_pairs={{0,96},{1,97},{2,98},{3,99},{4,100},{5,101},{6,102},{7,103},{8,104... | collective-permute-start | bytes 491528 | tf_op jit(solution)/shard_map/ppermute | solution.py:591
  23.6 3.2 collective-permute-start.14
  26.8 2.8 collective-permute-done.13.refs_14_
  29.6 3.0 collective-permute-start.12
  32.9 3.4 collective-permute-start.5
  36.3 3.0 collective-permute-start.8
  41.0 4.6 %collective-permute-done.5.refs_4_ = bf16[4,64,768]{2,1,0:T(8,128)(2,1)} collective-permute-done((bf16[4,64,768]{2,1,0:T(8,128)(2,1)}, bf16[4,64,768]{2,1,0:T(8,128)(2,1)}, u32[]{:S(2)}, u32[]{:S(2)}) %collective-permute-start.5) | collective-permute-done | bytes 393248 | tf_op jit(solution)/shard_map/ppermute | solution.py:591
  47.1 3.2 collective-permute-done.8.refs_7_
  50.2 6.9 %collective-permute-done.6.refs_5_ = bf16[4,64,768]{2,1,0:T(8,128)(2,1)} collective-permute-done((bf16[4,64,768]{2,1,0:T(8,128)(2,1)}, bf16[4,64,768]{2,1,0:T(8,128)(2,1)}, u32[]{:S(2)}, u32[]{:S(2)}) %collective-permute-start.6) | collective-permute-done | bytes 393248 | tf_op jit(solution)/shard_map/ppermute | solution.py:591
  57.1 6.2 %relay.1 = (bf16[4,64,1024]{2,1,0:T(8,128)(2,1)}, bf16[4,64,1024]{2,1,0:T(8,128)(2,1)}, bf16[4,64,1024]{2,1,0:T(8,128)(2,1)}, bf16[4,64,1024]{2,1,0:T(8,128)(2,1...) custom-call(s32[1]{0:T(128)} %bitcast.4.at_ref, ...), custom_call_target="tpu_custom_call" | custom-call | tf_op jit(solution)/shard_map/relay/pallas_call | solution.py:186
  63.3 2.7 collective-permute-start.15
  71.6 8.3 %collective-permute-done.15.refs_2_ = bf16[4,64,1024]{2,1,0:T(8,128)(2,1)S(1)} collective-permute-done((bf16[4,64,1024]{2,1,0:T(8,128)(2,1)}, bf16[4,64,1024]{2,1,0:T(8,128)(2,1)S(1)}, u32[]{:S(2)}, u32[]{:S(2)}) %collective-permute-start.15) | collective-permute-done | bytes 524320 | tf_op jit(solution)/shard_map/ppermute | solution.py:591
  87.2 2.7 collective-permute-done.17.refs_4_
  95.2 6.8 %collective-permute-done.19.refs_6_ = bf16[4,64,1024]{2,1,0:T(8,128)(2,1)} collective-permute-done((bf16[4,64,1024]{2,1,0:T(8,128)(2,1)}, bf16[4,64,1024]{2,1,0:T(8,128)(2,1)}, u32[]{:S(2)}, u32[]{:S(2)}) %collective-permute-start.19) | collective-permute-done | bytes 524320 | tf_op jit(solution)/shard_map/ppermute | solution.py:591
  103.9 7.4 %collective-permute-done.21.refs_8_ = bf16[4,64,1024]{2,1,0:T(8,128)(2,1)} collective-permute-done((bf16[4,64,1024]{2,1,0:T(8,128)(2,1)}, bf16[4,64,1024]{2,1,0:T(8,128)(2,1)}, u32[]{:S(2)}, u32[]{:S(2)}) %collective-permute-start.21) | collective-permute-done | bytes 524320 | tf_op jit(solution)/shard_map/ppermute | solution.py:591
  116.2 3.7 %collective-permute-done.25.refs_12_ = bf16[4,64,1024]{2,1,0:T(8,128)(2,1)} collective-permute-done((bf16[4,64,1024]{2,1,0:T(8,128)(2,1)}, bf16[4,64,1024]{2,1,0:T(8,128)(2,1)}, u32[]{:S(2)}, u32[]{:S(2)}) %collective-permute-start.25) | collective-permute-done | bytes 524320 | tf_op jit(solution)/shard_map/ppermute | solution.py:591
  119.9 5.9 %collective-permute-done.26.refs_13_ = bf16[4,64,1024]{2,1,0:T(8,128)(2,1)} collective-permute-done((bf16[4,64,1024]{2,1,0:T(8,128)(2,1)}, bf16[4,64,1024]{2,1,0:T(8,128)(2,1)}, u32[]{:S(2)}, u32[]{:S(2)}) %collective-permute-start.26) | collective-permute-done | bytes 524320 | tf_op jit(solution)/shard_map/ppermute | solution.py:591
  125.8 9.4 %shard_map.46 = (bf16[40,512,128]{2,1,0:T(8,128)(2,1)}, f32[2,128,256]{2,1,0:T(8,128)}, f32[2,128,256]{2,1,0:T(8,128)}, f32[2,128,256]{2,1,0:T(8,128)}, f32[2,128,256]{2,1,0:T(8,128)}) custom-call(s32[142]{0:T(256)} %concatenate.3.sc_ref, s32[1]{0:T(128)} %bitcast.my_ref, bf16[2048,768]{1,0:T(8,128)(2,1)} %fusion.1.unit_ref, ...), custom_call_target="tpu_custom_call" | custom-call | flops 6000000000 | bytes 12582912 | tf_op jit(solution)/shard_map/pallas_call | solution.py:377
  135.3 11.0 %shard_map.47 = (bf16[40,512,128]{2,1,0:T(8,128)(2,1)}, f32[2,128,256]{2,1,0:T(8,128)}, f32[2,128,256]{2,1,0:T(8,128)}, f32[2,128,256]{2,1,0:T(8,128)}, f32[2,128,256]{2,1,0:T(8,128)}) custom-call(s32[142]{0:T(256)} %concatenate.3.sc_ref, s32[1]{0:T(128)} %bitcast.my_ref, bf16[2048,768]{1,0:T(8,128)(2,1)} %fusion.1.unit_ref, ...), custom_call_target="tpu_custom_call" | custom-call | flops 6000000000 | bytes 12582912 | tf_op jit(solution)/shard_map/pallas_call | solution.py:377
  148.5 2.5 collective-permute-start.34
  153.3 2.5 collective-permute-done.32.refs_5_
  156.5 5.1 %collective-permute-done.33.refs_6_ = f32[256,256]{1,0:T(8,128)S(1)} collective-permute-done((f32[256,256]{1,0:T(8,128)}, f32[256,256]{1,0:T(8,128)S(1)}, u32[]{:S(2)}, u32[]{:S(2)}) %collective-permute-start.33) | collective-permute-done | bytes 262176 | tf_op jit(solution)/shard_map/ppermute | solution.py:591
  161.6 3.1 collective-permute-done.34.refs_7_
  167.0 3.8 %collective-permute-done.30.refs_2_ = f32[256,256]{1,0:T(8,128)S(1)} collective-permute-done((f32[256,256]{1,0:T(8,128)S(1)}, f32[256,256]{1,0:T(8,128)S(1)}, u32[]{:S(2)}, u32[]{:S(2)}) %collective-permute-start.30) | collective-permute-done | bytes 262176 | tf_op jit(solution)/shard_map/ppermute | solution.py:591
  170.8 2.5 collective-permute-done.31.refs_3_
  174.1 3.0 gram.2
  177.0 4.0 %collective-permute-start.36 = (f32[64,256]{1,0:T(8,128)}, f32[64,256]{1,0:T(8,128)S(1)}, u32[]{:S(2)}, u32[]{:S(2)}) collective-permute-start(f32[64,256]{1,0:T(8,128)} %get-tuple-element.157), channel_id=1, source_target_pairs={{0,2},{1,3},{2,0},{3,1},{4,6},{5,7},{6,4},{7,5},{8,10},{9,11},{10,... | collective-permute-start | bytes 196616 | tf_op jit(solution)/shard_map/ppermute | solution.py:591
  181.7 2.5 collective-permute-done.36
  184.2 2.5 collective-permute-done.37
  188.1 2.5 collective-permute-start.39
  204.6 3.0 collective-permute-start.45
  211.5 12.3 %step.1 = (bf16[4,128,256]{2,1,0:T(8,128)(2,1)}, bf16[32,128,256]{2,1,0:T(8,128)(2,1)}) custom-call(s32[1]{0:T(128)} %bitcast.my_ref, s32[32]{0:T(128)} %bitcast.29, f32[64,256]{1,0:T(8,128)} %copy-done.18, f32[64,256]{1,0:T(8,128)} %copy-done.30, f32[64,256]{1,0:T(8,128)} %copy-done.29, f32[64,256]{1,0:T(8,128)} %copy-done.28, ...), custom_call_target="tpu_custom_call" | custom-call | tf_op jit(solution)/shard_map/step/pallas_call | solution.py:536
  223.8 33.7 %all_to_all.5.refs_0_.refs_1_.refs_2_.refs_3_ = bf16[32,128,256]{2,1,0:T(8,128)(2,1)} all-to-all(bf16[32,128,256]{2,1,0:T(8,128)(2,1)} %get-tuple-element.160), channel_id=1, replica_groups=mesh['blk'=32,'vec'=4] {'blk'}, dimensions={0} | all-to-all | bytes 4194304 | tf_op jit(solution)/shard_map/all_to_all | solution.py:594
  257.5 6.0 %shard_map.48 = (f32[2,128,256]{2,1,0:T(8,128)}, f32[2,128,256]{2,1,0:T(8,128)}, f32[2,128,256]{2,1,0:T(8,128)}, f32[2,128,256]{2,1,0:T(8,128)}) custom-call(s32[142]{0:T(256)} %concatenate.3.sc_ref, s32[1]{0:T(128)} %bitcast.my_ref, bf16[40,512,128]{2,1,0:T(8,128)(2,1)} %get-tuple-element.146.aff_ref, ...), custom_call_target="tpu_custom_call" | custom-call | flops 2000000000 | bytes 12582912 | tf_op jit(solution)/shard_map/pallas_call | solution.py:400
  263.6 7.1 %shard_map.49 = (f32[2,128,256]{2,1,0:T(8,128)}, f32[2,128,256]{2,1,0:T(8,128)}, f32[2,128,256]{2,1,0:T(8,128)}, f32[2,128,256]{2,1,0:T(8,128)}) custom-call(s32[142]{0:T(256)} %concatenate.3.sc_ref, s32[1]{0:T(128)} %bitcast.my_ref, bf16[40,512,128]{2,1,0:T(8,128)(2,1)} %get-tuple-element.171.aff_ref, ...), custom_call_target="tpu_custom_call" | custom-call | flops 2000000000 | bytes 12582912 | tf_op jit(solution)/shard_map/pallas_call | solution.py:400
  275.3 3.4 collective-permute-start.49
  282.0 5.1 %collective-permute-done.52.refs_6_ = f32[256,256]{1,0:T(8,128)S(1)} collective-permute-done((f32[256,256]{1,0:T(8,128)}, f32[256,256]{1,0:T(8,128)S(1)}, u32[]{:S(2)}, u32[]{:S(2)}) %collective-permute-start.52) | collective-permute-done | bytes 262176 | tf_op jit(solution)/shard_map/ppermute | solution.py:591
  287.1 3.1 collective-permute-done.53.refs_7_
  291.3 5.1 %collective-permute-done.49.refs_2_ = f32[256,256]{1,0:T(8,128)S(1)} collective-permute-done((f32[256,256]{1,0:T(8,128)S(1)}, f32[256,256]{1,0:T(8,128)S(1)}, u32[]{:S(2)}, u32[]{:S(2)}) %collective-permute-start.49) | collective-permute-done | bytes 262176 | tf_op jit(solution)/shard_map/ppermute | solution.py:591
  296.4 2.5 collective-permute-done.50.refs_3_
  299.6 3.0 gram.3
  302.6 2.7 collective-permute-start.55
  327.3 2.8 collective-permute-done.61
  333.8 11.6 %collective-permute-done.66.refs_3_ = f32[64,256]{1,0:T(8,128)S(1)} collective-permute-done((f32[64,256]{1,0:T(8,128)S(1)}, f32[64,256]{1,0:T(8,128)S(1)}, u32[]{:S(2)}, u32[]{:S(2)}) %collective-permute-start.66) | collective-permute-done | bytes 65568 | tf_op jit(solution)/shard_map/ppermute | solution.py:591
  346.6 3.1 collective-permute-done.64.refs_1_
  351.5 12.7 %last.1 = f32[64,2048]{1,0:T(8,128)} custom-call(s32[1]{0:T(128)} %bitcast.my_ref, f32[64,256]{1,0:T(8,128)} %copy-done.17, f32[64,256]{1,0:T(8,128)} %copy-done.27, f32[64,256]{1,0:T(8,128)} %copy-done.26, f32[64,256]{1,0:T(8,128)} %copy-done.25, f32[512,256]{1,0:T(8,128)} %get-tuple-element.186.refs_4_, f32[512,256]{1,0:T(8,128)} %copy-done.3, ...), custom_call_target="tpu_custom_call" | custom-call | tf_op jit(solution)/shard_map/last/pallas_call | solution.py:572
  (219 shorter events, 106.0 us)
Async XLA Ops:
  2.0 7.1 %collective-permute-start = (bf16[64,512]{1,0:T(8,128)(2,1)}, bf16[64,512]{1,0:T(8,128)(2,1)S(1)}, u32[]{:S(2)}, u32[]{:S(2)}) collective-permute-start(bf16[64,512]{1,0:T(8,128)(2,1)} %get-tuple-element.104), channel_id=1, source_target_pairs={{0,1},{1,0},{2,3},{3,2},{4,5},{5,4},{6,7},{7,6},{8,9},{9,8},{10,11... | collective-permute-start | bytes 196616 | tf_op jit(solution)/shard_map/ppermute | solution.py:591
  12.6 28.2 %collective-permute-start.7 = (bf16[4,64,768]{2,1,0:T(8,128)(2,1)}, bf16[4,64,768]{2,1,0:T(8,128)(2,1)S(1)}, u32[]{:S(2)}, u32[]{:S(2)}) collective-permute-start(bf16[4,64,768]{2,1,0:T(8,128)(2,1)} %get-tuple-element.107.refs_0_), channel_id=1, source_target_pairs={{0,64},{1,65},{2,66},{3,67},{4,68},{5,69},{6,70},{7,71},{8,72},{9,... | collective-permute-start | bytes 1179656 | tf_op jit(solution)/shard_map/ppermute | solution.py:591
  19.9 9.7 %collective-permute-start.13 = (bf16[4,80,256]{2,1,0:T(8,128)(2,1)}, bf16[4,80,256]{2,1,0:T(8,128)(2,1)S(1)}, u32[]{:S(2)}, u32[]{:S(2)}) collective-permute-start(bf16[4,80,256]{2,1,0:T(8,128)(2,1)} %get-tuple-element.113.refs_8_), channel_id=1, source_target_pairs={{0,64},{1,65},{2,66},{3,67},{4,68},{5,69},{6,70},{7,71},{8,72},{9,... | collective-permute-start | bytes 491528 | tf_op jit(solution)/shard_map/ppermute | solution.py:591
  19.9 12.7 %collective-permute-start.11 = (bf16[4,80,256]{2,1,0:T(8,128)(2,1)}, bf16[4,80,256]{2,1,0:T(8,128)(2,1)S(1)}, u32[]{:S(2)}, u32[]{:S(2)}) collective-permute-start(bf16[4,80,256]{2,1,0:T(8,128)(2,1)} %get-tuple-element.113.refs_8_), channel_id=1, source_target_pairs={{0,96},{1,97},{2,98},{3,99},{4,100},{5,101},{6,102},{7,103},{8,104... | collective-permute-start | bytes 491528 | tf_op jit(solution)/shard_map/ppermute | solution.py:591
  23.6 9.3 %collective-permute-start.9 = (bf16[4,80,256]{2,1,0:T(8,128)(2,1)}, bf16[4,80,256]{2,1,0:T(8,128)(2,1)S(1)}, u32[]{:S(2)}, u32[]{:S(2)}) collective-permute-start(bf16[4,80,256]{2,1,0:T(8,128)(2,1)} %get-tuple-element.113.refs_8_), channel_id=1, source_target_pairs={{0,32},{1,33},{2,34},{3,35},{4,36},{5,37},{6,38},{7,39},{8,40},{9,... | collective-permute-start | bytes 491528 | tf_op jit(solution)/shard_map/ppermute | solution.py:591
  23.6 12.7 %collective-permute-start.14 = (bf16[4,80,256]{2,1,0:T(8,128)(2,1)}, bf16[4,80,256]{2,1,0:T(8,128)(2,1)S(1)}, u32[]{:S(2)}, u32[]{:S(2)}) collective-permute-start(bf16[4,80,256]{2,1,0:T(8,128)(2,1)} %get-tuple-element.114.refs_9_), channel_id=1, source_target_pairs={{0,16},{1,17},{2,18},{3,19},{4,20},{5,21},{6,22},{7,23},{8,24},{9,... | collective-permute-start | bytes 491528 | tf_op jit(solution)/shard_map/ppermute | solution.py:591
  29.6 6.7 %collective-permute-start.12 = (bf16[4,80,256]{2,1,0:T(8,128)(2,1)}, bf16[4,80,256]{2,1,0:T(8,128)(2,1)S(1)}, u32[]{:S(2)}, u32[]{:S(2)}) collective-permute-start(bf16[4,80,256]{2,1,0:T(8,128)(2,1)} %get-tuple-element.114.refs_9_), channel_id=1, source_target_pairs={{0,24},{1,25},{2,26},{3,27},{4,28},{5,29},{6,30},{7,31},{8,16},{9,... | collective-permute-start | bytes 491528 | tf_op jit(solution)/shard_map/ppermute | solution.py:591
  32.6 6.7 %collective-permute-start.10 = (bf16[4,80,256]{2,1,0:T(8,128)(2,1)}, bf16[4,80,256]{2,1,0:T(8,128)(2,1)S(1)}, u32[]{:S(2)}, u32[]{:S(2)}) collective-permute-start(bf16[4,80,256]{2,1,0:T(8,128)(2,1)} %get-tuple-element.114.refs_9_), channel_id=1, source_target_pairs={{0,8},{1,9},{2,10},{3,11},{4,12},{5,13},{6,14},{7,15},{8,0},{9,1},... | collective-permute-start | bytes 491528 | tf_op jit(solution)/shard_map/ppermute | solution.py:591
  32.9 12.7 %collective-permute-start.5 = (bf16[4,64,768]{2,1,0:T(8,128)(2,1)}, bf16[4,64,768]{2,1,0:T(8,128)(2,1)}, u32[]{:S(2)}, u32[]{:S(2)}) collective-permute-start(bf16[4,64,768]{2,1,0:T(8,128)(2,1)} %get-tuple-element.107.refs_0_), channel_id=1, source_target_pairs={{0,96},{1,97},{2,98},{3,99},{4,100},{5,101},{6,102},{7,103},{8,104... | collective-permute-start | bytes 1179656 | tf_op jit(solution)/shard_map/ppermute | solution.py:591
  36.3 10.8 %collective-permute-start.3 = (bf16[4,64,768]{2,1,0:T(8,128)(2,1)}, bf16[4,64,768]{2,1,0:T(8,128)(2,1)}, u32[]{:S(2)}, u32[]{:S(2)}) collective-permute-start(bf16[4,64,768]{2,1,0:T(8,128)(2,1)} %get-tuple-element.107.refs_0_), channel_id=1, source_target_pairs={{0,32},{1,33},{2,34},{3,35},{4,36},{5,37},{6,38},{7,39},{8,40},{9,... | collective-permute-start | bytes 1179656 | tf_op jit(solution)/shard_map/ppermute | solution.py:591
  36.3 13.9 %collective-permute-start.8 = (bf16[4,64,768]{2,1,0:T(8,128)(2,1)}, bf16[4,64,768]{2,1,0:T(8,128)(2,1)}, u32[]{:S(2)}, u32[]{:S(2)}) collective-permute-start(bf16[4,64,768]{2,1,0:T(8,128)(2,1)} %get-tuple-element.108.refs_1_), channel_id=1, source_target_pairs={{0,16},{1,17},{2,18},{3,19},{4,20},{5,21},{6,22},{7,23},{8,24},{9,... | collective-permute-start | bytes 1179656 | tf_op jit(solution)/shard_map/ppermute | solution.py:591
  39.3 17.8 %collective-permute-start.6 = (bf16[4,64,768]{2,1,0:T(8,128)(2,1)}, bf16[4,64,768]{2,1,0:T(8,128)(2,1)}, u32[]{:S(2)}, u32[]{:S(2)}) collective-permute-start(bf16[4,64,768]{2,1,0:T(8,128)(2,1)} %get-tuple-element.108.refs_1_), channel_id=1, source_target_pairs={{0,24},{1,25},{2,26},{3,27},{4,28},{5,29},{6,30},{7,31},{8,16},{9,... | collective-permute-start | bytes 1179656 | tf_op jit(solution)/shard_map/ppermute | solution.py:591
  40.9 16.2 %collective-permute-start.4 = (bf16[4,64,768]{2,1,0:T(8,128)(2,1)}, bf16[4,64,768]{2,1,0:T(8,128)(2,1)}, u32[]{:S(2)}, u32[]{:S(2)}) collective-permute-start(bf16[4,64,768]{2,1,0:T(8,128)(2,1)} %get-tuple-element.108.refs_1_), channel_id=1, source_target_pairs={{0,8},{1,9},{2,10},{3,11},{4,12},{5,13},{6,14},{7,15},{8,0},{9,1},... | collective-permute-start | bytes 1179656 | tf_op jit(solution)/shard_map/ppermute | solution.py:591
  63.3 16.6 %collective-permute-start.15 = (bf16[4,64,1024]{2,1,0:T(8,128)(2,1)}, bf16[4,64,1024]{2,1,0:T(8,128)(2,1)S(1)}, u32[]{:S(2)}, u32[]{:S(2)}) collective-permute-start(bf16[4,64,1024]{2,1,0:T(8,128)(2,1)} %get-tuple-element.115), channel_id=1, source_target_pairs={{0,16},{1,17},{2,18},{3,19},{4,20},{5,21},{6,22},{7,23},{8,24},{9,... | collective-permute-start | bytes 1572872 | tf_op jit(solution)/shard_map/ppermute | solution.py:591
  66.0 21.1 %collective-permute-start.16 = (bf16[4,64,1024]{2,1,0:T(8,128)(2,1)}, bf16[4,64,1024]{2,1,0:T(8,128)(2,1)}, u32[]{:S(2)}, u32[]{:S(2)}) collective-permute-start(bf16[4,64,1024]{2,1,0:T(8,128)(2,1)} %get-tuple-element.122), channel_id=1, source_target_pairs={{0,64},{1,65},{2,66},{3,67},{4,68},{5,69},{6,70},{7,71},{8,72},{9,... | collective-permute-start | bytes 1572872 | tf_op jit(solution)/shard_map/ppermute | solution.py:591
  67.8 22.1 %collective-permute-start.17 = (bf16[4,64,1024]{2,1,0:T(8,128)(2,1)}, bf16[4,64,1024]{2,1,0:T(8,128)(2,1)}, u32[]{:S(2)}, u32[]{:S(2)}) collective-permute-start(bf16[4,64,1024]{2,1,0:T(8,128)(2,1)} %get-tuple-element.123), channel_id=1, source_target_pairs={{0,20},{1,21},{2,22},{3,23},{4,16},{5,17},{6,18},{7,19},{8,28},{9,... | collective-permute-start | bytes 1572872 | tf_op jit(solution)/shard_map/ppermute | solution.py:591
  69.1 23.2 %collective-permute-start.18 = (bf16[4,64,1024]{2,1,0:T(8,128)(2,1)}, bf16[4,64,1024]{2,1,0:T(8,128)(2,1)}, u32[]{:S(2)}, u32[]{:S(2)}) collective-permute-start(bf16[4,64,1024]{2,1,0:T(8,128)(2,1)} %get-tuple-element.124), channel_id=1, source_target_pairs={{0,68},{1,69},{2,70},{3,71},{4,64},{5,65},{6,66},{7,67},{8,76},{9,... | collective-permute-start | bytes 1572872 | tf_op jit(solution)/shard_map/ppermute | solution.py:591
  70.2 31.8 %collective-permute-start.19 = (bf16[4,64,1024]{2,1,0:T(8,128)(2,1)}, bf16[4,64,1024]{2,1,0:T(8,128)(2,1)}, u32[]{:S(2)}, u32[]{:S(2)}) collective-permute-start(bf16[4,64,1024]{2,1,0:T(8,128)(2,1)} %get-tuple-element.125), channel_id=1, source_target_pairs={{0,8},{1,9},{2,10},{3,11},{4,12},{5,13},{6,14},{7,15},{8,0},{9,1},... | collective-permute-start | bytes 1572872 | tf_op jit(solution)/shard_map/ppermute | solution.py:591
  79.9 24.0 %collective-permute-start.20 = (bf16[4,64,1024]{2,1,0:T(8,128)(2,1)}, bf16[4,64,1024]{2,1,0:T(8,128)(2,1)}, u32[]{:S(2)}, u32[]{:S(2)}) collective-permute-start(bf16[4,64,1024]{2,1,0:T(8,128)(2,1)} %get-tuple-element.126), channel_id=1, source_target_pairs={{0,32},{1,33},{2,34},{3,35},{4,36},{5,37},{6,38},{7,39},{8,40},{9,... | collective-permute-start | bytes 1572872 | tf_op jit(solution)/shard_map/ppermute | solution.py:591
  87.2 24.2 %collective-permute-start.21 = (bf16[4,64,1024]{2,1,0:T(8,128)(2,1)}, bf16[4,64,1024]{2,1,0:T(8,128)(2,1)}, u32[]{:S(2)}, u32[]{:S(2)}) collective-permute-start(bf16[4,64,1024]{2,1,0:T(8,128)(2,1)} %get-tuple-element.127), channel_id=1, source_target_pairs={{0,12},{1,13},{2,14},{3,15},{4,8},{5,9},{6,10},{7,11},{8,4},{9,5},... | collective-permute-start | bytes 1572872 | tf_op jit(solution)/shard_map/ppermute | solution.py:591
  89.9 23.5 %collective-permute-start.22 = (bf16[4,64,1024]{2,1,0:T(8,128)(2,1)}, bf16[4,64,1024]{2,1,0:T(8,128)(2,1)}, u32[]{:S(2)}, u32[]{:S(2)}) collective-permute-start(bf16[4,64,1024]{2,1,0:T(8,128)(2,1)} %get-tuple-element.128), channel_id=1, source_target_pairs={{0,36},{1,37},{2,38},{3,39},{4,32},{5,33},{6,34},{7,35},{8,44},{9,... | collective-permute-start | bytes 1572872 | tf_op jit(solution)/shard_map/ppermute | solution.py:591
  92.3 21.6 %collective-permute-start.23 = (bf16[4,64,1024]{2,1,0:T(8,128)(2,1)}, bf16[4,64,1024]{2,1,0:T(8,128)(2,1)}, u32[]{:S(2)}, u32[]{:S(2)}) collective-permute-start(bf16[4,64,1024]{2,1,0:T(8,128)(2,1)} %get-tuple-element.129), channel_id=1, source_target_pairs={{0,24},{1,25},{2,26},{3,27},{4,28},{5,29},{6,30},{7,31},{8,16},{9,... | collective-permute-start | bytes 1572872 | tf_op jit(solution)/shard_map/ppermute | solution.py:591
  102.0 14.2 %collective-permute-start.24 = (bf16[4,64,1024]{2,1,0:T(8,128)(2,1)}, bf16[4,64,1024]{2,1,0:T(8,128)(2,1)}, u32[]{:S(2)}, u32[]{:S(2)}) collective-permute-start(bf16[4,64,1024]{2,1,0:T(8,128)(2,1)} %get-tuple-element.130), channel_id=1, source_target_pairs={{0,96},{1,97},{2,98},{3,99},{4,100},{5,101},{6,102},{7,103},{8,104... | collective-permute-start | bytes 1572872 | tf_op jit(solution)/shard_map/ppermute | solution.py:591
  103.9 16.0 %collective-permute-start.25 = (bf16[4,64,1024]{2,1,0:T(8,128)(2,1)}, bf16[4,64,1024]{2,1,0:T(8,128)(2,1)}, u32[]{:S(2)}, u32[]{:S(2)}) collective-permute-start(bf16[4,64,1024]{2,1,0:T(8,128)(2,1)} %get-tuple-element.131), channel_id=1, source_target_pairs={{0,28},{1,29},{2,30},{3,31},{4,24},{5,25},{6,26},{7,27},{8,20},{9,... | collective-permute-start | bytes 1572872 | tf_op jit(solution)/shard_map/ppermute | solution.py:591
  111.3 14.5 %collective-permute-start.26 = (bf16[4,64,1024]{2,1,0:T(8,128)(2,1)}, bf16[4,64,1024]{2,1,0:T(8,128)(2,1)}, u32[]{:S(2)}, u32[]{:S(2)}) collective-permute-start(bf16[4,64,1024]{2,1,0:T(8,128)(2,1)} %get-tuple-element.132), channel_id=1, source_target_pairs={{0,100},{1,101},{2,102},{3,103},{4,96},{5,97},{6,98},{7,99},{8,108... | collective-permute-start | bytes 1572872 | tf_op jit(solution)/shard_map/ppermute | solution.py:591
  113.4 12.4 %collective-permute-start.27 = (bf16[4,64,1024]{2,1,0:T(8,128)(2,1)}, bf16[4,64,1024]{2,1,0:T(8,128)(2,1)}, u32[]{:S(2)}, u32[]{:S(2)}) collective-permute-start(bf16[4,64,1024]{2,1,0:T(8,128)(2,1)} %get-tuple-element.133), channel_id=1, source_target_pairs={{0,4},{1,5},{2,6},{3,7},{4,0},{5,1},{6,2},{7,3},{8,12},{9,13},{10,... | collective-permute-start | bytes 1572872 | tf_op jit(solution)/shard_map/ppermute | solution.py:591
  113.9 11.9 %collective-permute-start.28 = (bf16[4,64,1024]{2,1,0:T(8,128)(2,1)}, bf16[4,64,1024]{2,1,0:T(8,128)(2,1)}, u32[]{:S(2)}, u32[]{:S(2)}) collective-permute-start(bf16[4,64,1024]{2,1,0:T(8,128)(2,1)} %get-tuple-element.134), channel_id=1, source_target_pairs={{0,4},{1,5},{2,6},{3,7},{4,0},{5,1},{6,2},{7,3},{8,12},{9,13},{10,... | collective-permute-start | bytes 1572872 | tf_op jit(solution)/shard_map/ppermute | solution.py:591
  146.3 9.5 %collective-permute-start.32 = (f32[256,256]{1,0:T(8,128)}, f32[256,256]{1,0:T(8,128)S(1)}, u32[]{:S(2)}, u32[]{:S(2)}) collective-permute-start(f32[256,256]{1,0:T(8,128)} %bitcast.43), channel_id=1, source_target_pairs={{0,1},{1,0},{2,3},{3,2},{4,5},{5,4},{6,7},{7,6},{8,9},{9,8},{10,11... | collective-permute-start | bytes 786440 | tf_op jit(solution)/shard_map/ppermute | solution.py:591
  146.4 15.2 %collective-permute-start.33 = (f32[256,256]{1,0:T(8,128)}, f32[256,256]{1,0:T(8,128)S(1)}, u32[]{:S(2)}, u32[]{:S(2)}) collective-permute-start(f32[256,256]{1,0:T(8,128)} %bitcast.42), channel_id=1, source_target_pairs={{0,2},{1,3},{2,0},{3,1},{4,6},{5,7},{6,4},{7,5},{8,10},{9,11},{10,... | collective-permute-start | bytes 786440 | tf_op jit(solution)/shard_map/ppermute | solution.py:591
  148.5 16.2 %collective-permute-start.34 = (f32[256,256]{1,0:T(8,128)}, f32[256,256]{1,0:T(8,128)S(1)}, u32[]{:S(2)}, u32[]{:S(2)}) collective-permute-start(f32[256,256]{1,0:T(8,128)} %bitcast.40), channel_id=1, source_target_pairs={{0,3},{1,2},{2,1},{3,0},{4,7},{5,6},{6,5},{7,4},{8,11},{9,10},{10,... | collective-permute-start | bytes 786440 | tf_op jit(solution)/shard_map/ppermute | solution.py:591
  151.1 16.0 %collective-permute-start.29 = (f32[256,256]{1,0:T(8,128)S(1)}, f32[256,256]{1,0:T(8,128)S(1)}, u32[]{:S(2)}, u32[]{:S(2)}) collective-permute-start(f32[256,256]{1,0:T(8,128)S(1)} %bitcast.37), channel_id=1, source_target_pairs={{0,1},{1,0},{2,3},{3,2},{4,5},{5,4},{6,7},{7,6},{8,9},{9,8},{10,11... | collective-permute-start | bytes 786440 | tf_op jit(solution)/shard_map/ppermute | solution.py:591
  151.1 19.8 %collective-permute-start.30 = (f32[256,256]{1,0:T(8,128)S(1)}, f32[256,256]{1,0:T(8,128)S(1)}, u32[]{:S(2)}, u32[]{:S(2)}) collective-permute-start(f32[256,256]{1,0:T(8,128)S(1)} %bitcast.36), channel_id=1, source_target_pairs={{0,2},{1,3},{2,0},{3,1},{4,6},{5,7},{6,4},{7,5},{8,10},{9,11},{10,... | collective-permute-start | bytes 786440 | tf_op jit(solution)/shard_map/ppermute | solution.py:591
  155.7 17.6 %collective-permute-start.31 = (f32[256,256]{1,0:T(8,128)S(1)}, f32[256,256]{1,0:T(8,128)S(1)}, u32[]{:S(2)}, u32[]{:S(2)}) collective-permute-start(f32[256,256]{1,0:T(8,128)S(1)} %bitcast.35), channel_id=1, source_target_pairs={{0,3},{1,2},{2,1},{3,0},{4,7},{5,6},{6,5},{7,4},{8,11},{9,10},{10,... | collective-permute-start | bytes 786440 | tf_op jit(solution)/shard_map/ppermute | solution.py:591
  177.0 7.2 %collective-permute-start.36 = (f32[64,256]{1,0:T(8,128)}, f32[64,256]{1,0:T(8,128)S(1)}, u32[]{:S(2)}, u32[]{:S(2)}) collective-permute-start(f32[64,256]{1,0:T(8,128)} %get-tuple-element.157), channel_id=1, source_target_pairs={{0,2},{1,3},{2,0},{3,1},{4,6},{5,7},{6,4},{7,5},{8,10},{9,11},{10,... | collective-permute-start | bytes 196616 | tf_op jit(solution)/shard_map/ppermute | solution.py:591
  203.4 6.5 %collective-permute-start.47 = (f32[64,256]{1,0:T(8,128)S(1)}, f32[64,256]{1,0:T(8,128)S(1)}, u32[]{:S(2)}, u32[]{:S(2)}) collective-permute-start(f32[64,256]{1,0:T(8,128)S(1)} %add.132.refs_0_), channel_id=1, source_target_pairs={{0,3},{1,2},{2,1},{3,0},{4,7},{5,6},{6,5},{7,4},{8,11},{9,10},{10,... | collective-permute-start | bytes 196616 | tf_op jit(solution)/shard_map/ppermute | solution.py:591
  204.6 6.2 %collective-permute-start.45 = (f32[64,256]{1,0:T(8,128)S(1)}, f32[64,256]{1,0:T(8,128)S(1)}, u32[]{:S(2)}, u32[]{:S(2)}) collective-permute-start(f32[64,256]{1,0:T(8,128)S(1)} %add.132.refs_0_), channel_id=1, source_target_pairs={{0,1},{1,0},{2,3},{3,2},{4,5},{5,4},{6,7},{7,6},{8,9},{9,8},{10,11... | collective-permute-start | bytes 196616 | tf_op jit(solution)/shard_map/ppermute | solution.py:591
  270.6 9.4 %collective-permute-start.51 = (f32[256,256]{1,0:T(8,128)}, f32[256,256]{1,0:T(8,128)S(1)}, u32[]{:S(2)}, u32[]{:S(2)}) collective-permute-start(f32[256,256]{1,0:T(8,128)} %bitcast.46), channel_id=1, source_target_pairs={{0,1},{1,0},{2,3},{3,2},{4,5},{5,4},{6,7},{7,6},{8,9},{9,8},{10,11... | collective-permute-start | bytes 786440 | tf_op jit(solution)/shard_map/ppermute | solution.py:591
  271.6 15.5 %collective-permute-start.52 = (f32[256,256]{1,0:T(8,128)}, f32[256,256]{1,0:T(8,128)S(1)}, u32[]{:S(2)}, u32[]{:S(2)}) collective-permute-start(f32[256,256]{1,0:T(8,128)} %bitcast.45), channel_id=1, source_target_pairs={{0,2},{1,3},{2,0},{3,1},{4,6},{5,7},{6,4},{7,5},{8,10},{9,11},{10,... | collective-permute-start | bytes 786440 | tf_op jit(solution)/shard_map/ppermute | solution.py:591
  274.1 16.2 %collective-permute-start.53 = (f32[256,256]{1,0:T(8,128)}, f32[256,256]{1,0:T(8,128)S(1)}, u32[]{:S(2)}, u32[]{:S(2)}) collective-permute-start(f32[256,256]{1,0:T(8,128)} %bitcast.44), channel_id=1, source_target_pairs={{0,3},{1,2},{2,1},{3,0},{4,7},{5,6},{6,5},{7,4},{8,11},{9,10},{10,... | collective-permute-start | bytes 786440 | tf_op jit(solution)/shard_map/ppermute | solution.py:591
  275.3 16.0 %collective-permute-start.48 = (f32[256,256]{1,0:T(8,128)S(1)}, f32[256,256]{1,0:T(8,128)S(1)}, u32[]{:S(2)}, u32[]{:S(2)}) collective-permute-start(f32[256,256]{1,0:T(8,128)S(1)} %bitcast.41), channel_id=1, source_target_pairs={{0,1},{1,0},{2,3},{3,2},{4,5},{5,4},{6,7},{7,6},{8,9},{9,8},{10,11... | collective-permute-start | bytes 786440 | tf_op jit(solution)/shard_map/ppermute | solution.py:591
  275.3 21.0 %collective-permute-start.49 = (f32[256,256]{1,0:T(8,128)S(1)}, f32[256,256]{1,0:T(8,128)S(1)}, u32[]{:S(2)}, u32[]{:S(2)}) collective-permute-start(f32[256,256]{1,0:T(8,128)S(1)} %bitcast.39), channel_id=1, source_target_pairs={{0,2},{1,3},{2,0},{3,1},{4,6},{5,7},{6,4},{7,5},{8,10},{9,11},{10,... | collective-permute-start | bytes 786440 | tf_op jit(solution)/shard_map/ppermute | solution.py:591
  280.0 18.9 %collective-permute-start.50 = (f32[256,256]{1,0:T(8,128)S(1)}, f32[256,256]{1,0:T(8,128)S(1)}, u32[]{:S(2)}, u32[]{:S(2)}) collective-permute-start(f32[256,256]{1,0:T(8,128)S(1)} %bitcast.38), channel_id=1, source_target_pairs={{0,3},{1,2},{2,1},{3,0},{4,7},{5,6},{6,5},{7,4},{8,11},{9,10},{10,... | collective-permute-start | bytes 786440 | tf_op jit(solution)/shard_map/ppermute | solution.py:591
  319.0 6.9 %collective-permute-start.62 = (f32[64,256]{1,0:T(8,128)S(1)}, f32[64,256]{1,0:T(8,128)S(1)}, u32[]{:S(2)}, u32[]{:S(2)}) collective-permute-start(f32[64,256]{1,0:T(8,128)S(1)} %add_add_fusion.1), channel_id=1, source_target_pairs={{0,96},{1,97},{2,98},{3,99},{4,100},{5,101},{6,102},{7,103},{8,104... | collective-permute-start | bytes 196616 | tf_op jit(solution)/shard_map/ppermute | solution.py:591
  320.3 29.4 %collective-permute-start.69 = (f32[512,256]{1,0:T(8,128)}, f32[512,256]{1,0:T(8,128)S(1)}, u32[]{:S(2)}, u32[]{:S(2)}) collective-permute-start(f32[512,256]{1,0:T(8,128)} %get-tuple-element.186.refs_4_), channel_id=1, source_target_pairs={{0,3},{1,2},{2,1},{3,0},{4,7},{5,6},{6,5},{7,4},{8,11},{9,10},{10,... | collective-permute-start | bytes 1572872 | tf_op jit(solution)/shard_map/ppermute | solution.py:591
  322.2 27.4 %collective-permute-start.68 = (f32[512,256]{1,0:T(8,128)}, f32[512,256]{1,0:T(8,128)S(1)}, u32[]{:S(2)}, u32[]{:S(2)}) collective-permute-start(f32[512,256]{1,0:T(8,128)} %get-tuple-element.186.refs_4_), channel_id=1, source_target_pairs={{0,2},{1,3},{2,0},{3,1},{4,6},{5,7},{6,4},{7,5},{8,10},{9,11},{10,... | collective-permute-start | bytes 1572872 | tf_op jit(solution)/shard_map/ppermute | solution.py:591
  322.2 27.5 %collective-permute-start.67 = (f32[512,256]{1,0:T(8,128)}, f32[512,256]{1,0:T(8,128)S(1)}, u32[]{:S(2)}, u32[]{:S(2)}) collective-permute-start(f32[512,256]{1,0:T(8,128)} %get-tuple-element.186.refs_4_), channel_id=1, source_target_pairs={{0,1},{1,0},{2,3},{3,2},{4,5},{5,4},{6,7},{7,6},{8,9},{9,8},{10,11... | collective-permute-start | bytes 1572872 | tf_op jit(solution)/shard_map/ppermute | solution.py:591
  331.6 13.8 %collective-permute-start.66 = (f32[64,256]{1,0:T(8,128)S(1)}, f32[64,256]{1,0:T(8,128)S(1)}, u32[]{:S(2)}, u32[]{:S(2)}) collective-permute-start(f32[64,256]{1,0:T(8,128)S(1)} %add.142.refs_0_), channel_id=1, source_target_pairs={{0,3},{1,2},{2,1},{3,0},{4,7},{5,6},{6,5},{7,4},{8,11},{9,10},{10,... | collective-permute-start | bytes 196616 | tf_op jit(solution)/shard_map/ppermute | solution.py:591
  333.7 12.9 %collective-permute-start.65 = (f32[64,256]{1,0:T(8,128)S(1)}, f32[64,256]{1,0:T(8,128)S(1)}, u32[]{:S(2)}, u32[]{:S(2)}) collective-permute-start(f32[64,256]{1,0:T(8,128)S(1)} %add.142.refs_0_), channel_id=1, source_target_pairs={{0,2},{1,3},{2,0},{3,1},{4,6},{5,7},{6,4},{7,5},{8,10},{9,11},{10,... | collective-permute-start | bytes 196616 | tf_op jit(solution)/shard_map/ppermute | solution.py:591
  (65 other events, 657.3 us)
where the time goes:
time: 365 us; the launch traced here: 364 us
  waiting for transfers between devices  137 us (38%)
  starting transfers between devices  100 us (27%)
  Pallas kernels  77.1 us (21%)
  blocking collectives  33.7 us (9%)
  local copies, waits for them, and re-layouts  7.04 us (2%)
  other arithmetic  6.99 us (2%)
    ppermute x70, waiting for transfers between devices, swap(): return lax.ppermute(x, AXES, perm)  137 us
    ppermute x70, starting transfers between devices, swap(): return lax.ppermute(x, AXES, perm)  100 us
    all_to_all x1, blocking collectives, exchange(): return lax.all_to_all(x, axis, split_axis=0, concat_axis=0, tiled=True)  33.7 us
    pallas_call x2, Pallas kernels, pairs_first(): pl.pallas_call(functools.partial(pairs_first_body, entries, part), out_sh...  20.4 us
    pallas_call x2, Pallas kernels, pairs_next(): pl.pallas_call(functools.partial(pairs_next_body, entries, part), out_sha...  13.1 us
    pallas_call x1, Pallas kernels, last(): pl.pallas_call(functools.partial(last_body, label_total, chunks), out_sha...  12.7 us
    pallas_call x1, Pallas kernels, step(): pl.pallas_call(functools.partial(step_body, label_total, chunks), out_sha...  12.3 us
  transfers between devices with their start and end apart: 70, of which 48 were waited for; matrix products, arithmetic and copies ran while one was open for 2% of the time, Pallas kernels for 1%

commit v1 on v0

--- a/solution.py
+++ b/solution.py
@@ -620,14 +620,18 @@
         owner = lax.axis_index("blk").astype(jnp.int32)
         cuts = cut_start(basis.T, my, nvec)
         x, cuts = lax.optimization_barrier((x, cuts))
-        vts = [cuts[0]] + [swap(cuts[d], 0, d) for d in range(1, nvec)]
+        vts = [cuts[0]]
+        for d in range(1, nvec):
+            vts.append(swap(cuts[d], 0, d))
         units = own_quarter(x, my, blocks, quarter)
-        units, vts = lax.optimization_barrier((units, vts))
 
         def along(x, h, d):
             return x if d == 0 else swap(x, d << SHIFT[LINES[h][0]], 0)
 
-        feats = [along(units[h], h, d) for d in STEPS for h in range(2)]
+        feats = []
+        for d in STEPS:
+            for h in range(2):
+                feats.append(along(units[h], h, d))
         vown, packs = send_start(vts, pb, my, blocks, quarter)
         vecs = [along(packs[h], h, d) for d in STEPS for h in range(2)]
         sends = relay(feats, vecs, owner[None])

time: 365 us -> 364 us (level)
  waiting for transfers between devices: 137 us -> 133 us
  transfers between devices with their start and end apart: 70 -> 70, of which waited for: 48 -> 45; matrix products, arithmetic and copies ran while one was open for 2% -> 2% of each run, Pallas kernels for 1% -> 1%
where the time goes in v1:
time: 364 us; the launch traced here: 363 us
  waiting for transfers between devices  133 us (37%)
  starting transfers between devices  103 us (28%)
  Pallas kernels  77 us (21%)
  blocking collectives  33.7 us (9%)
  other arithmetic  6.98 us (2%)
  local copies, waits for them, and re-layouts  6.39 us (2%)
    ppermute x70, waiting for transfers between devices, swap(): return lax.ppermute(x, AXES, perm)  133 us
    ppermute x70, starting transfers between devices, swap(): return lax.ppermute(x, AXES, perm)  103 us
    all_to_all x1, blocking collectives, exchange(): return lax.all_to_all(x, axis, split_axis=0, concat_axis=0, tiled=True)  33.7 us
    pallas_call x2, Pallas kernels, pairs_first(): pl.pallas_call(functools.partial(pairs_first_body, entries, part), out_sh...  20.3 us
    pallas_call x2, Pallas kernels, pairs_next(): pl.pallas_call(functools.partial(pairs_next_body, entries, part), out_sha...  13 us
    pallas_call x1, Pallas kernels, last(): pl.pallas_call(functools.partial(last_body, label_total, chunks), out_sha...  12.7 us
    pallas_call x1, Pallas kernels, step(): pl.pallas_call(functools.partial(step_body, label_total, chunks), out_sha...  12.3 us
  transfers between devices with their start and end apart: 70, of which 45 were waited for; matrix products, arithmetic and copies ran while one was open for 2% of the time, Pallas kernels for 1%

profile of v1, /device:TPU:0, one launch (start us, length us, event | category | flops | bytes accessed | tf_op | source)
XLA Modules:
  0.0 362.8 jit_solution(357124042147141422)
XLA Ops:
  3.6 2.7 collective-permute-start.7
  9.1 4.1 %collective-permute-start.4 = (bf16[4,64,768]{2,1,0:T(8,128)(2,1)}, bf16[4,64,768]{2,1,0:T(8,128)(2,1)S(1)}, u32[]{:S(2)}, u32[]{:S(2)}) collective-permute-start(bf16[4,64,768]{2,1,0:T(8,128)(2,1)} %get-tuple-element.95.refs_0_), channel_id=1, source_target_pairs={{0,64},{1,65},{2,66},{3,67},{4,68},{5,69},{6,70},{7,71},{8,72},{9,... | collective-permute-start | bytes 1179656 | tf_op jit(solution)/shard_map/ppermute | solution.py:591
  20.2 3.2 collective-permute-start.14
  23.4 3.5 collective-permute-done.13.refs_14_
  26.9 3.0 collective-permute-start.12
  30.3 3.4 collective-permute-start.2
  33.7 3.0 collective-permute-start.5
  38.4 4.6 %collective-permute-done.2.refs_4_ = bf16[4,64,768]{2,1,0:T(8,128)(2,1)} collective-permute-done((bf16[4,64,768]{2,1,0:T(8,128)(2,1)}, bf16[4,64,768]{2,1,0:T(8,128)(2,1)}, u32[]{:S(2)}, u32[]{:S(2)}) %collective-permute-start.2) | collective-permute-done | bytes 393248 | tf_op jit(solution)/shard_map/ppermute | solution.py:591
  44.5 3.2 collective-permute-done.5.refs_7_
  47.6 6.9 %collective-permute-done.3.refs_5_ = bf16[4,64,768]{2,1,0:T(8,128)(2,1)} collective-permute-done((bf16[4,64,768]{2,1,0:T(8,128)(2,1)}, bf16[4,64,768]{2,1,0:T(8,128)(2,1)}, u32[]{:S(2)}, u32[]{:S(2)}) %collective-permute-start.3) | collective-permute-done | bytes 393248 | tf_op jit(solution)/shard_map/ppermute | solution.py:591
  54.5 6.2 %relay.1 = (bf16[4,64,1024]{2,1,0:T(8,128)(2,1)}, bf16[4,64,1024]{2,1,0:T(8,128)(2,1)}, bf16[4,64,1024]{2,1,0:T(8,128)(2,1)}, bf16[4,64,1024]{2,1,0:T(8,128)(2,1...) custom-call(s32[1]{0:T(128)} %bitcast.4.at_ref, ...), custom_call_target="tpu_custom_call" | custom-call | tf_op jit(solution)/shard_map/relay/pallas_call | solution.py:186
  60.7 2.7 collective-permute-start.15
  69.0 8.3 %collective-permute-done.15.refs_2_ = bf16[4,64,1024]{2,1,0:T(8,128)(2,1)S(1)} collective-permute-done((bf16[4,64,1024]{2,1,0:T(8,128)(2,1)}, bf16[4,64,1024]{2,1,0:T(8,128)(2,1)S(1)}, u32[]{:S(2)}, u32[]{:S(2)}) %collective-permute-start.15) | collective-permute-done | bytes 524320 | tf_op jit(solution)/shard_map/ppermute | solution.py:591
  84.4 2.9 collective-permute-done.17.refs_4_
  92.6 6.8 %collective-permute-done.19.refs_6_ = bf16[4,64,1024]{2,1,0:T(8,128)(2,1)} collective-permute-done((bf16[4,64,1024]{2,1,0:T(8,128)(2,1)}, bf16[4,64,1024]{2,1,0:T(8,128)(2,1)}, u32[]{:S(2)}, u32[]{:S(2)}) %collective-permute-start.19) | collective-permute-done | bytes 524320 | tf_op jit(solution)/shard_map/ppermute | solution.py:591
  101.3 7.4 %collective-permute-done.21.refs_8_ = bf16[4,64,1024]{2,1,0:T(8,128)(2,1)} collective-permute-done((bf16[4,64,1024]{2,1,0:T(8,128)(2,1)}, bf16[4,64,1024]{2,1,0:T(8,128)(2,1)}, u32[]{:S(2)}, u32[]{:S(2)}) %collective-permute-start.21) | collective-permute-done | bytes 524320 | tf_op jit(solution)/shard_map/ppermute | solution.py:591
  113.6 3.7 %collective-permute-done.25.refs_12_ = bf16[4,64,1024]{2,1,0:T(8,128)(2,1)} collective-permute-done((bf16[4,64,1024]{2,1,0:T(8,128)(2,1)}, bf16[4,64,1024]{2,1,0:T(8,128)(2,1)}, u32[]{:S(2)}, u32[]{:S(2)}) %collective-permute-start.25) | collective-permute-done | bytes 524320 | tf_op jit(solution)/shard_map/ppermute | solution.py:591
  117.3 5.9 %collective-permute-done.26.refs_13_ = bf16[4,64,1024]{2,1,0:T(8,128)(2,1)} collective-permute-done((bf16[4,64,1024]{2,1,0:T(8,128)(2,1)}, bf16[4,64,1024]{2,1,0:T(8,128)(2,1)}, u32[]{:S(2)}, u32[]{:S(2)}) %collective-permute-start.26) | collective-permute-done | bytes 524320 | tf_op jit(solution)/shard_map/ppermute | solution.py:591
  123.2 9.4 %shard_map.46 = (bf16[40,512,128]{2,1,0:T(8,128)(2,1)}, f32[2,128,256]{2,1,0:T(8,128)}, f32[2,128,256]{2,1,0:T(8,128)}, f32[2,128,256]{2,1,0:T(8,128)}, f32[2,128,256]{2,1,0:T(8,128)}) custom-call(s32[142]{0:T(256)} %concatenate.3.sc_ref, s32[1]{0:T(128)} %bitcast.my_ref, bf16[2048,768]{1,0:T(8,128)(2,1)} %fusion.1.unit_ref, ...), custom_call_target="tpu_custom_call" | custom-call | flops 6000000000 | bytes 12582912 | tf_op jit(solution)/shard_map/pallas_call | solution.py:377
  132.7 10.9 %shard_map.47 = (bf16[40,512,128]{2,1,0:T(8,128)(2,1)}, f32[2,128,256]{2,1,0:T(8,128)}, f32[2,128,256]{2,1,0:T(8,128)}, f32[2,128,256]{2,1,0:T(8,128)}, f32[2,128,256]{2,1,0:T(8,128)}) custom-call(s32[142]{0:T(256)} %concatenate.3.sc_ref, s32[1]{0:T(128)} %bitcast.my_ref, bf16[2048,768]{1,0:T(8,128)(2,1)} %fusion.1.unit_ref, ...), custom_call_target="tpu_custom_call" | custom-call | flops 6000000000 | bytes 12582912 | tf_op jit(solution)/shard_map/pallas_call | solution.py:377
  144.0 3.9 %collective-permute-start.33 = (f32[256,256]{1,0:T(8,128)}, f32[256,256]{1,0:T(8,128)S(1)}, u32[]{:S(2)}, u32[]{:S(2)}) collective-permute-start(f32[256,256]{1,0:T(8,128)} %bitcast.42), channel_id=1, source_target_pairs={{0,2},{1,3},{2,0},{3,1},{4,6},{5,7},{6,4},{7,5},{8,10},{9,11},{10,... | collective-permute-start | bytes 786440 | tf_op jit(solution)/shard_map/ppermute | solution.py:591
  148.4 4.2 %collective-permute-start.30 = (f32[256,256]{1,0:T(8,128)S(1)}, f32[256,256]{1,0:T(8,128)S(1)}, u32[]{:S(2)}, u32[]{:S(2)}) collective-permute-start(f32[256,256]{1,0:T(8,128)S(1)} %bitcast.36), channel_id=1, source_target_pairs={{0,2},{1,3},{2,0},{3,1},{4,6},{5,7},{6,4},{7,5},{8,10},{9,11},{10,... | collective-permute-start | bytes 786440 | tf_op jit(solution)/shard_map/ppermute | solution.py:591
  153.1 2.8 collective-permute-start.31
  155.8 5.1 %collective-permute-done.33.refs_6_ = f32[256,256]{1,0:T(8,128)S(1)} collective-permute-done((f32[256,256]{1,0:T(8,128)}, f32[256,256]{1,0:T(8,128)S(1)}, u32[]{:S(2)}, u32[]{:S(2)}) %collective-permute-start.33) | collective-permute-done | bytes 262176 | tf_op jit(solution)/shard_map/ppermute | solution.py:591
  160.9 3.1 collective-permute-done.34.refs_7_
  164.3 5.9 %collective-permute-done.30.refs_2_ = f32[256,256]{1,0:T(8,128)S(1)} collective-permute-done((f32[256,256]{1,0:T(8,128)S(1)}, f32[256,256]{1,0:T(8,128)S(1)}, u32[]{:S(2)}, u32[]{:S(2)}) %collective-permute-start.30) | collective-permute-done | bytes 262176 | tf_op jit(solution)/shard_map/ppermute | solution.py:591
  170.2 2.5 collective-permute-done.31.refs_3_
  173.4 3.0 gram.2
  178.3 2.8 collective-permute-start.37
  200.7 2.8 collective-permute-start.47
  206.7 3.0 collective-permute-done.46.refs_2_
  210.3 12.3 %step.1 = (bf16[4,128,256]{2,1,0:T(8,128)(2,1)}, bf16[32,128,256]{2,1,0:T(8,128)(2,1)}) custom-call(s32[1]{0:T(128)} %bitcast.my_ref, s32[32]{0:T(128)} %bitcast.29, f32[64,256]{1,0:T(8,128)} %copy-done.18, f32[64,256]{1,0:T(8,128)} %copy-done.30, f32[64,256]{1,0:T(8,128)} %copy-done.29, f32[64,256]{1,0:T(8,128)} %copy-done.28, ...), custom_call_target="tpu_custom_call" | custom-call | tf_op jit(solution)/shard_map/step/pallas_call | solution.py:536
  222.6 33.7 %all_to_all.5.refs_0_.refs_1_.refs_2_.refs_3_ = bf16[32,128,256]{2,1,0:T(8,128)(2,1)} all-to-all(bf16[32,128,256]{2,1,0:T(8,128)(2,1)} %get-tuple-element.148), channel_id=1, replica_groups=mesh['blk'=32,'vec'=4] {'blk'}, dimensions={0} | all-to-all | bytes 4194304 | tf_op jit(solution)/shard_map/all_to_all | solution.py:594
  256.4 6.0 %shard_map.48 = (f32[2,128,256]{2,1,0:T(8,128)}, f32[2,128,256]{2,1,0:T(8,128)}, f32[2,128,256]{2,1,0:T(8,128)}, f32[2,128,256]{2,1,0:T(8,128)}) custom-call(s32[142]{0:T(256)} %concatenate.3.sc_ref, s32[1]{0:T(128)} %bitcast.my_ref, bf16[40,512,128]{2,1,0:T(8,128)(2,1)} %get-tuple-element.134.aff_ref, ...), custom_call_target="tpu_custom_call" | custom-call | flops 2000000000 | bytes 12582912 | tf_op jit(solution)/shard_map/pallas_call | solution.py:400
  262.4 7.0 %shard_map.49 = (f32[2,128,256]{2,1,0:T(8,128)}, f32[2,128,256]{2,1,0:T(8,128)}, f32[2,128,256]{2,1,0:T(8,128)}, f32[2,128,256]{2,1,0:T(8,128)}) custom-call(s32[142]{0:T(256)} %concatenate.3.sc_ref, s32[1]{0:T(128)} %bitcast.my_ref, bf16[40,512,128]{2,1,0:T(8,128)(2,1)} %get-tuple-element.159.aff_ref, ...), custom_call_target="tpu_custom_call" | custom-call | flops 2000000000 | bytes 12582912 | tf_op jit(solution)/shard_map/pallas_call | solution.py:400
  269.4 2.7 collective-permute-start.52
  274.1 2.7 collective-permute-start.49
  280.1 5.1 %collective-permute-done.52.refs_6_ = f32[256,256]{1,0:T(8,128)S(1)} collective-permute-done((f32[256,256]{1,0:T(8,128)}, f32[256,256]{1,0:T(8,128)S(1)}, u32[]{:S(2)}, u32[]{:S(2)}) %collective-permute-start.52) | collective-permute-done | bytes 262176 | tf_op jit(solution)/shard_map/ppermute | solution.py:591
  285.2 3.1 collective-permute-done.53.refs_7_
  290.1 4.3 %collective-permute-done.49.refs_2_ = f32[256,256]{1,0:T(8,128)S(1)} collective-permute-done((f32[256,256]{1,0:T(8,128)S(1)}, f32[256,256]{1,0:T(8,128)S(1)}, u32[]{:S(2)}, u32[]{:S(2)}) %collective-permute-start.49) | collective-permute-done | bytes 262176 | tf_op jit(solution)/shard_map/ppermute | solution.py:591
  294.4 2.5 collective-permute-done.50.refs_3_
  297.7 3.0 gram.3
  300.6 3.5 collective-permute-start.55
  320.3 2.9 collective-permute-start.67
  326.1 2.9 collective-permute-done.61
  332.6 11.5 %collective-permute-done.66.refs_3_ = f32[64,256]{1,0:T(8,128)S(1)} collective-permute-done((f32[64,256]{1,0:T(8,128)S(1)}, f32[64,256]{1,0:T(8,128)S(1)}, u32[]{:S(2)}, u32[]{:S(2)}) %collective-permute-start.66) | collective-permute-done | bytes 65568 | tf_op jit(solution)/shard_map/ppermute | solution.py:591
  344.9 3.5 collective-permute-done.64.refs_1_
  350.1 12.7 %last.1 = f32[64,2048]{1,0:T(8,128)} custom-call(s32[1]{0:T(128)} %bitcast.my_ref, f32[64,256]{1,0:T(8,128)} %copy-done.17, f32[64,256]{1,0:T(8,128)} %copy-done.27, f32[64,256]{1,0:T(8,128)} %copy-done.26, f32[64,256]{1,0:T(8,128)} %copy-done.25, f32[512,256]{1,0:T(8,128)} %get-tuple-element.174.refs_4_, f32[512,256]{1,0:T(8,128)} %copy-done.3, ...), custom_call_target="tpu_custom_call" | custom-call | tf_op jit(solution)/shard_map/last/pallas_call | solution.py:572
  (213 shorter events, 100.4 us)
Async XLA Ops:
  2.0 11.9 %collective-permute-start.6 = (bf16[64,512]{1,0:T(8,128)(2,1)}, bf16[64,512]{1,0:T(8,128)(2,1)}, u32[]{:S(2)}, u32[]{:S(2)}) collective-permute-start(bf16[64,512]{1,0:T(8,128)(2,1)} %get-tuple-element.98), channel_id=1, source_target_pairs={{0,1},{1,0},{2,3},{3,2},{4,5},{5,4},{6,7},{7,6},{8,9},{9,8},{10,11... | collective-permute-start | bytes 196616 | tf_op jit(solution)/shard_map/ppermute | solution.py:591
  3.6 10.3 %collective-permute-start.7 = (bf16[64,512]{1,0:T(8,128)(2,1)}, bf16[64,512]{1,0:T(8,128)(2,1)}, u32[]{:S(2)}, u32[]{:S(2)}) collective-permute-start(bf16[64,512]{1,0:T(8,128)(2,1)} %get-tuple-element.99), channel_id=1, source_target_pairs={{0,2},{1,3},{2,0},{3,1},{4,6},{5,7},{6,4},{7,5},{8,10},{9,11},{10,... | collective-permute-start | bytes 196616 | tf_op jit(solution)/shard_map/ppermute | solution.py:591
  6.3 7.5 %collective-permute-start.8 = (bf16[64,512]{1,0:T(8,128)(2,1)}, bf16[64,512]{1,0:T(8,128)(2,1)}, u32[]{:S(2)}, u32[]{:S(2)}) collective-permute-start(bf16[64,512]{1,0:T(8,128)(2,1)} %get-tuple-element.100), channel_id=1, source_target_pairs={{0,3},{1,2},{2,1},{3,0},{4,7},{5,6},{6,5},{7,4},{8,11},{9,10},{10,... | collective-permute-start | bytes 196616 | tf_op jit(solution)/shard_map/ppermute | solution.py:591
  9.1 29.1 %collective-permute-start.4 = (bf16[4,64,768]{2,1,0:T(8,128)(2,1)}, bf16[4,64,768]{2,1,0:T(8,128)(2,1)S(1)}, u32[]{:S(2)}, u32[]{:S(2)}) collective-permute-start(bf16[4,64,768]{2,1,0:T(8,128)(2,1)} %get-tuple-element.95.refs_0_), channel_id=1, source_target_pairs={{0,64},{1,65},{2,66},{3,67},{4,68},{5,69},{6,70},{7,71},{8,72},{9,... | collective-permute-start | bytes 1179656 | tf_op jit(solution)/shard_map/ppermute | solution.py:591
  16.5 10.4 %collective-permute-start.13 = (bf16[4,80,256]{2,1,0:T(8,128)(2,1)}, bf16[4,80,256]{2,1,0:T(8,128)(2,1)S(1)}, u32[]{:S(2)}, u32[]{:S(2)}) collective-permute-start(bf16[4,80,256]{2,1,0:T(8,128)(2,1)} %get-tuple-element.101.refs_8_), channel_id=1, source_target_pairs={{0,64},{1,65},{2,66},{3,67},{4,68},{5,69},{6,70},{7,71},{8,72},{9,... | collective-permute-start | bytes 491528 | tf_op jit(solution)/shard_map/ppermute | solution.py:591
  18.7 11.3 %collective-permute-start.11 = (bf16[4,80,256]{2,1,0:T(8,128)(2,1)}, bf16[4,80,256]{2,1,0:T(8,128)(2,1)S(1)}, u32[]{:S(2)}, u32[]{:S(2)}) collective-permute-start(bf16[4,80,256]{2,1,0:T(8,128)(2,1)} %get-tuple-element.101.refs_8_), channel_id=1, source_target_pairs={{0,96},{1,97},{2,98},{3,99},{4,100},{5,101},{6,102},{7,103},{8,104... | collective-permute-start | bytes 491528 | tf_op jit(solution)/shard_map/ppermute | solution.py:591
  20.2 10.0 %collective-permute-start.9 = (bf16[4,80,256]{2,1,0:T(8,128)(2,1)}, bf16[4,80,256]{2,1,0:T(8,128)(2,1)S(1)}, u32[]{:S(2)}, u32[]{:S(2)}) collective-permute-start(bf16[4,80,256]{2,1,0:T(8,128)(2,1)} %get-tuple-element.101.refs_8_), channel_id=1, source_target_pairs={{0,32},{1,33},{2,34},{3,35},{4,36},{5,37},{6,38},{7,39},{8,40},{9,... | collective-permute-start | bytes 491528 | tf_op jit(solution)/shard_map/ppermute | solution.py:591
  20.2 13.4 %collective-permute-start.14 = (bf16[4,80,256]{2,1,0:T(8,128)(2,1)}, bf16[4,80,256]{2,1,0:T(8,128)(2,1)S(1)}, u32[]{:S(2)}, u32[]{:S(2)}) collective-permute-start(bf16[4,80,256]{2,1,0:T(8,128)(2,1)} %get-tuple-element.102.refs_9_), channel_id=1, source_target_pairs={{0,16},{1,17},{2,18},{3,19},{4,20},{5,21},{6,22},{7,23},{8,24},{9,... | collective-permute-start | bytes 491528 | tf_op jit(solution)/shard_map/ppermute | solution.py:591
  26.9 6.8 %collective-permute-start.12 = (bf16[4,80,256]{2,1,0:T(8,128)(2,1)}, bf16[4,80,256]{2,1,0:T(8,128)(2,1)S(1)}, u32[]{:S(2)}, u32[]{:S(2)}) collective-permute-start(bf16[4,80,256]{2,1,0:T(8,128)(2,1)} %get-tuple-element.102.refs_9_), channel_id=1, source_target_pairs={{0,24},{1,25},{2,26},{3,27},{4,28},{5,29},{6,30},{7,31},{8,16},{9,... | collective-permute-start | bytes 491528 | tf_op jit(solution)/shard_map/ppermute | solution.py:591
  29.9 6.8 %collective-permute-start.10 = (bf16[4,80,256]{2,1,0:T(8,128)(2,1)}, bf16[4,80,256]{2,1,0:T(8,128)(2,1)S(1)}, u32[]{:S(2)}, u32[]{:S(2)}) collective-permute-start(bf16[4,80,256]{2,1,0:T(8,128)(2,1)} %get-tuple-element.102.refs_9_), channel_id=1, source_target_pairs={{0,8},{1,9},{2,10},{3,11},{4,12},{5,13},{6,14},{7,15},{8,0},{9,1},... | collective-permute-start | bytes 491528 | tf_op jit(solution)/shard_map/ppermute | solution.py:591
  30.3 12.7 %collective-permute-start.2 = (bf16[4,64,768]{2,1,0:T(8,128)(2,1)}, bf16[4,64,768]{2,1,0:T(8,128)(2,1)}, u32[]{:S(2)}, u32[]{:S(2)}) collective-permute-start(bf16[4,64,768]{2,1,0:T(8,128)(2,1)} %get-tuple-element.95.refs_0_), channel_id=1, source_target_pairs={{0,96},{1,97},{2,98},{3,99},{4,100},{5,101},{6,102},{7,103},{8,104... | collective-permute-start | bytes 1179656 | tf_op jit(solution)/shard_map/ppermute | solution.py:591
  33.7 10.8 %collective-permute-start = (bf16[4,64,768]{2,1,0:T(8,128)(2,1)}, bf16[4,64,768]{2,1,0:T(8,128)(2,1)}, u32[]{:S(2)}, u32[]{:S(2)}) collective-permute-start(bf16[4,64,768]{2,1,0:T(8,128)(2,1)} %get-tuple-element.95.refs_0_), channel_id=1, source_target_pairs={{0,32},{1,33},{2,34},{3,35},{4,36},{5,37},{6,38},{7,39},{8,40},{9,... | collective-permute-start | bytes 1179656 | tf_op jit(solution)/shard_map/ppermute | solution.py:591
  33.7 13.9 %collective-permute-start.5 = (bf16[4,64,768]{2,1,0:T(8,128)(2,1)}, bf16[4,64,768]{2,1,0:T(8,128)(2,1)}, u32[]{:S(2)}, u32[]{:S(2)}) collective-permute-start(bf16[4,64,768]{2,1,0:T(8,128)(2,1)} %get-tuple-element.96.refs_1_), channel_id=1, source_target_pairs={{0,16},{1,17},{2,18},{3,19},{4,20},{5,21},{6,22},{7,23},{8,24},{9,... | collective-permute-start | bytes 1179656 | tf_op jit(solution)/shard_map/ppermute | solution.py:591
  36.7 17.8 %collective-permute-start.3 = (bf16[4,64,768]{2,1,0:T(8,128)(2,1)}, bf16[4,64,768]{2,1,0:T(8,128)(2,1)}, u32[]{:S(2)}, u32[]{:S(2)}) collective-permute-start(bf16[4,64,768]{2,1,0:T(8,128)(2,1)} %get-tuple-element.96.refs_1_), channel_id=1, source_target_pairs={{0,24},{1,25},{2,26},{3,27},{4,28},{5,29},{6,30},{7,31},{8,16},{9,... | collective-permute-start | bytes 1179656 | tf_op jit(solution)/shard_map/ppermute | solution.py:591
  38.3 16.2 %collective-permute-start.1 = (bf16[4,64,768]{2,1,0:T(8,128)(2,1)}, bf16[4,64,768]{2,1,0:T(8,128)(2,1)}, u32[]{:S(2)}, u32[]{:S(2)}) collective-permute-start(bf16[4,64,768]{2,1,0:T(8,128)(2,1)} %get-tuple-element.96.refs_1_), channel_id=1, source_target_pairs={{0,8},{1,9},{2,10},{3,11},{4,12},{5,13},{6,14},{7,15},{8,0},{9,1},... | collective-permute-start | bytes 1179656 | tf_op jit(solution)/shard_map/ppermute | solution.py:591
  60.7 16.6 %collective-permute-start.15 = (bf16[4,64,1024]{2,1,0:T(8,128)(2,1)}, bf16[4,64,1024]{2,1,0:T(8,128)(2,1)S(1)}, u32[]{:S(2)}, u32[]{:S(2)}) collective-permute-start(bf16[4,64,1024]{2,1,0:T(8,128)(2,1)} %get-tuple-element.103), channel_id=1, source_target_pairs={{0,16},{1,17},{2,18},{3,19},{4,20},{5,21},{6,22},{7,23},{8,24},{9,... | collective-permute-start | bytes 1572872 | tf_op jit(solution)/shard_map/ppermute | solution.py:591
  63.4 21.0 %collective-permute-start.16 = (bf16[4,64,1024]{2,1,0:T(8,128)(2,1)}, bf16[4,64,1024]{2,1,0:T(8,128)(2,1)}, u32[]{:S(2)}, u32[]{:S(2)}) collective-permute-start(bf16[4,64,1024]{2,1,0:T(8,128)(2,1)} %get-tuple-element.110), channel_id=1, source_target_pairs={{0,64},{1,65},{2,66},{3,67},{4,68},{5,69},{6,70},{7,71},{8,72},{9,... | collective-permute-start | bytes 1572872 | tf_op jit(solution)/shard_map/ppermute | solution.py:591
  65.2 22.1 %collective-permute-start.17 = (bf16[4,64,1024]{2,1,0:T(8,128)(2,1)}, bf16[4,64,1024]{2,1,0:T(8,128)(2,1)}, u32[]{:S(2)}, u32[]{:S(2)}) collective-permute-start(bf16[4,64,1024]{2,1,0:T(8,128)(2,1)} %get-tuple-element.111), channel_id=1, source_target_pairs={{0,20},{1,21},{2,22},{3,23},{4,16},{5,17},{6,18},{7,19},{8,28},{9,... | collective-permute-start | bytes 1572872 | tf_op jit(solution)/shard_map/ppermute | solution.py:591
  66.5 23.2 %collective-permute-start.18 = (bf16[4,64,1024]{2,1,0:T(8,128)(2,1)}, bf16[4,64,1024]{2,1,0:T(8,128)(2,1)}, u32[]{:S(2)}, u32[]{:S(2)}) collective-permute-start(bf16[4,64,1024]{2,1,0:T(8,128)(2,1)} %get-tuple-element.112), channel_id=1, source_target_pairs={{0,68},{1,69},{2,70},{3,71},{4,64},{5,65},{6,66},{7,67},{8,76},{9,... | collective-permute-start | bytes 1572872 | tf_op jit(solution)/shard_map/ppermute | solution.py:591
  67.6 31.8 %collective-permute-start.19 = (bf16[4,64,1024]{2,1,0:T(8,128)(2,1)}, bf16[4,64,1024]{2,1,0:T(8,128)(2,1)}, u32[]{:S(2)}, u32[]{:S(2)}) collective-permute-start(bf16[4,64,1024]{2,1,0:T(8,128)(2,1)} %get-tuple-element.113), channel_id=1, source_target_pairs={{0,8},{1,9},{2,10},{3,11},{4,12},{5,13},{6,14},{7,15},{8,0},{9,1},... | collective-permute-start | bytes 1572872 | tf_op jit(solution)/shard_map/ppermute | solution.py:591
  77.3 24.0 %collective-permute-start.20 = (bf16[4,64,1024]{2,1,0:T(8,128)(2,1)}, bf16[4,64,1024]{2,1,0:T(8,128)(2,1)}, u32[]{:S(2)}, u32[]{:S(2)}) collective-permute-start(bf16[4,64,1024]{2,1,0:T(8,128)(2,1)} %get-tuple-element.114), channel_id=1, source_target_pairs={{0,32},{1,33},{2,34},{3,35},{4,36},{5,37},{6,38},{7,39},{8,40},{9,... | collective-permute-start | bytes 1572872 | tf_op jit(solution)/shard_map/ppermute | solution.py:591
  84.4 24.4 %collective-permute-start.21 = (bf16[4,64,1024]{2,1,0:T(8,128)(2,1)}, bf16[4,64,1024]{2,1,0:T(8,128)(2,1)}, u32[]{:S(2)}, u32[]{:S(2)}) collective-permute-start(bf16[4,64,1024]{2,1,0:T(8,128)(2,1)} %get-tuple-element.115), channel_id=1, source_target_pairs={{0,12},{1,13},{2,14},{3,15},{4,8},{5,9},{6,10},{7,11},{8,4},{9,5},... | collective-permute-start | bytes 1572872 | tf_op jit(solution)/shard_map/ppermute | solution.py:591
  87.3 23.5 %collective-permute-start.22 = (bf16[4,64,1024]{2,1,0:T(8,128)(2,1)}, bf16[4,64,1024]{2,1,0:T(8,128)(2,1)}, u32[]{:S(2)}, u32[]{:S(2)}) collective-permute-start(bf16[4,64,1024]{2,1,0:T(8,128)(2,1)} %get-tuple-element.116), channel_id=1, source_target_pairs={{0,36},{1,37},{2,38},{3,39},{4,32},{5,33},{6,34},{7,35},{8,44},{9,... | collective-permute-start | bytes 1572872 | tf_op jit(solution)/shard_map/ppermute | solution.py:591
  89.7 21.6 %collective-permute-start.23 = (bf16[4,64,1024]{2,1,0:T(8,128)(2,1)}, bf16[4,64,1024]{2,1,0:T(8,128)(2,1)}, u32[]{:S(2)}, u32[]{:S(2)}) collective-permute-start(bf16[4,64,1024]{2,1,0:T(8,128)(2,1)} %get-tuple-element.117), channel_id=1, source_target_pairs={{0,24},{1,25},{2,26},{3,27},{4,28},{5,29},{6,30},{7,31},{8,16},{9,... | collective-permute-start | bytes 1572872 | tf_op jit(solution)/shard_map/ppermute | solution.py:591
  99.4 14.2 %collective-permute-start.24 = (bf16[4,64,1024]{2,1,0:T(8,128)(2,1)}, bf16[4,64,1024]{2,1,0:T(8,128)(2,1)}, u32[]{:S(2)}, u32[]{:S(2)}) collective-permute-start(bf16[4,64,1024]{2,1,0:T(8,128)(2,1)} %get-tuple-element.118), channel_id=1, source_target_pairs={{0,96},{1,97},{2,98},{3,99},{4,100},{5,101},{6,102},{7,103},{8,104... | collective-permute-start | bytes 1572872 | tf_op jit(solution)/shard_map/ppermute | solution.py:591
  101.3 16.0 %collective-permute-start.25 = (bf16[4,64,1024]{2,1,0:T(8,128)(2,1)}, bf16[4,64,1024]{2,1,0:T(8,128)(2,1)}, u32[]{:S(2)}, u32[]{:S(2)}) collective-permute-start(bf16[4,64,1024]{2,1,0:T(8,128)(2,1)} %get-tuple-element.119), channel_id=1, source_target_pairs={{0,28},{1,29},{2,30},{3,31},{4,24},{5,25},{6,26},{7,27},{8,20},{9,... | collective-permute-start | bytes 1572872 | tf_op jit(solution)/shard_map/ppermute | solution.py:591
  108.7 14.5 %collective-permute-start.26 = (bf16[4,64,1024]{2,1,0:T(8,128)(2,1)}, bf16[4,64,1024]{2,1,0:T(8,128)(2,1)}, u32[]{:S(2)}, u32[]{:S(2)}) collective-permute-start(bf16[4,64,1024]{2,1,0:T(8,128)(2,1)} %get-tuple-element.120), channel_id=1, source_target_pairs={{0,100},{1,101},{2,102},{3,103},{4,96},{5,97},{6,98},{7,99},{8,108... | collective-permute-start | bytes 1572872 | tf_op jit(solution)/shard_map/ppermute | solution.py:591
  110.8 12.4 %collective-permute-start.27 = (bf16[4,64,1024]{2,1,0:T(8,128)(2,1)}, bf16[4,64,1024]{2,1,0:T(8,128)(2,1)}, u32[]{:S(2)}, u32[]{:S(2)}) collective-permute-start(bf16[4,64,1024]{2,1,0:T(8,128)(2,1)} %get-tuple-element.121), channel_id=1, source_target_pairs={{0,4},{1,5},{2,6},{3,7},{4,0},{5,1},{6,2},{7,3},{8,12},{9,13},{10,... | collective-permute-start | bytes 1572872 | tf_op jit(solution)/shard_map/ppermute | solution.py:591
  111.3 11.9 %collective-permute-start.28 = (bf16[4,64,1024]{2,1,0:T(8,128)(2,1)}, bf16[4,64,1024]{2,1,0:T(8,128)(2,1)}, u32[]{:S(2)}, u32[]{:S(2)}) collective-permute-start(bf16[4,64,1024]{2,1,0:T(8,128)(2,1)} %get-tuple-element.122), channel_id=1, source_target_pairs={{0,4},{1,5},{2,6},{3,7},{4,0},{5,1},{6,2},{7,3},{8,12},{9,13},{10,... | collective-permute-start | bytes 1572872 | tf_op jit(solution)/shard_map/ppermute | solution.py:591
  143.6 9.5 %collective-permute-start.32 = (f32[256,256]{1,0:T(8,128)}, f32[256,256]{1,0:T(8,128)S(1)}, u32[]{:S(2)}, u32[]{:S(2)}) collective-permute-start(f32[256,256]{1,0:T(8,128)} %bitcast.43), channel_id=1, source_target_pairs={{0,1},{1,0},{2,3},{3,2},{4,5},{5,4},{6,7},{7,6},{8,9},{9,8},{10,11... | collective-permute-start | bytes 786440 | tf_op jit(solution)/shard_map/ppermute | solution.py:591
  144.0 17.0 %collective-permute-start.33 = (f32[256,256]{1,0:T(8,128)}, f32[256,256]{1,0:T(8,128)S(1)}, u32[]{:S(2)}, u32[]{:S(2)}) collective-permute-start(f32[256,256]{1,0:T(8,128)} %bitcast.42), channel_id=1, source_target_pairs={{0,2},{1,3},{2,0},{3,1},{4,6},{5,7},{6,4},{7,5},{8,10},{9,11},{10,... | collective-permute-start | bytes 786440 | tf_op jit(solution)/shard_map/ppermute | solution.py:591
  147.9 16.2 %collective-permute-start.34 = (f32[256,256]{1,0:T(8,128)}, f32[256,256]{1,0:T(8,128)S(1)}, u32[]{:S(2)}, u32[]{:S(2)}) collective-permute-start(f32[256,256]{1,0:T(8,128)} %bitcast.40), channel_id=1, source_target_pairs={{0,3},{1,2},{2,1},{3,0},{4,7},{5,6},{6,5},{7,4},{8,11},{9,10},{10,... | collective-permute-start | bytes 786440 | tf_op jit(solution)/shard_map/ppermute | solution.py:591
  148.4 16.0 %collective-permute-start.29 = (f32[256,256]{1,0:T(8,128)S(1)}, f32[256,256]{1,0:T(8,128)S(1)}, u32[]{:S(2)}, u32[]{:S(2)}) collective-permute-start(f32[256,256]{1,0:T(8,128)S(1)} %bitcast.37), channel_id=1, source_target_pairs={{0,1},{1,0},{2,3},{3,2},{4,5},{5,4},{6,7},{7,6},{8,9},{9,8},{10,11... | collective-permute-start | bytes 786440 | tf_op jit(solution)/shard_map/ppermute | solution.py:591
  148.4 21.8 %collective-permute-start.30 = (f32[256,256]{1,0:T(8,128)S(1)}, f32[256,256]{1,0:T(8,128)S(1)}, u32[]{:S(2)}, u32[]{:S(2)}) collective-permute-start(f32[256,256]{1,0:T(8,128)S(1)} %bitcast.36), channel_id=1, source_target_pairs={{0,2},{1,3},{2,0},{3,1},{4,6},{5,7},{6,4},{7,5},{8,10},{9,11},{10,... | collective-permute-start | bytes 786440 | tf_op jit(solution)/shard_map/ppermute | solution.py:591
  153.1 19.7 %collective-permute-start.31 = (f32[256,256]{1,0:T(8,128)S(1)}, f32[256,256]{1,0:T(8,128)S(1)}, u32[]{:S(2)}, u32[]{:S(2)}) collective-permute-start(f32[256,256]{1,0:T(8,128)S(1)} %bitcast.35), channel_id=1, source_target_pairs={{0,3},{1,2},{2,1},{3,0},{4,7},{5,6},{6,5},{7,4},{8,11},{9,10},{10,... | collective-permute-start | bytes 786440 | tf_op jit(solution)/shard_map/ppermute | solution.py:591
  269.4 9.4 %collective-permute-start.51 = (f32[256,256]{1,0:T(8,128)}, f32[256,256]{1,0:T(8,128)S(1)}, u32[]{:S(2)}, u32[]{:S(2)}) collective-permute-start(f32[256,256]{1,0:T(8,128)} %bitcast.46), channel_id=1, source_target_pairs={{0,1},{1,0},{2,3},{3,2},{4,5},{5,4},{6,7},{7,6},{8,9},{9,8},{10,11... | collective-permute-start | bytes 786440 | tf_op jit(solution)/shard_map/ppermute | solution.py:591
  269.4 15.7 %collective-permute-start.52 = (f32[256,256]{1,0:T(8,128)}, f32[256,256]{1,0:T(8,128)S(1)}, u32[]{:S(2)}, u32[]{:S(2)}) collective-permute-start(f32[256,256]{1,0:T(8,128)} %bitcast.45), channel_id=1, source_target_pairs={{0,2},{1,3},{2,0},{3,1},{4,6},{5,7},{6,4},{7,5},{8,10},{9,11},{10,... | collective-permute-start | bytes 786440 | tf_op jit(solution)/shard_map/ppermute | solution.py:591
  272.1 16.2 %collective-permute-start.53 = (f32[256,256]{1,0:T(8,128)}, f32[256,256]{1,0:T(8,128)S(1)}, u32[]{:S(2)}, u32[]{:S(2)}) collective-permute-start(f32[256,256]{1,0:T(8,128)} %bitcast.44), channel_id=1, source_target_pairs={{0,3},{1,2},{2,1},{3,0},{4,7},{5,6},{6,5},{7,4},{8,11},{9,10},{10,... | collective-permute-start | bytes 786440 | tf_op jit(solution)/shard_map/ppermute | solution.py:591
  274.1 16.0 %collective-permute-start.48 = (f32[256,256]{1,0:T(8,128)S(1)}, f32[256,256]{1,0:T(8,128)S(1)}, u32[]{:S(2)}, u32[]{:S(2)}) collective-permute-start(f32[256,256]{1,0:T(8,128)S(1)} %bitcast.41), channel_id=1, source_target_pairs={{0,1},{1,0},{2,3},{3,2},{4,5},{5,4},{6,7},{7,6},{8,9},{9,8},{10,11... | collective-permute-start | bytes 786440 | tf_op jit(solution)/shard_map/ppermute | solution.py:591
  274.1 20.3 %collective-permute-start.49 = (f32[256,256]{1,0:T(8,128)S(1)}, f32[256,256]{1,0:T(8,128)S(1)}, u32[]{:S(2)}, u32[]{:S(2)}) collective-permute-start(f32[256,256]{1,0:T(8,128)S(1)} %bitcast.39), channel_id=1, source_target_pairs={{0,2},{1,3},{2,0},{3,1},{4,6},{5,7},{6,4},{7,5},{8,10},{9,11},{10,... | collective-permute-start | bytes 786440 | tf_op jit(solution)/shard_map/ppermute | solution.py:591
  278.8 18.1 %collective-permute-start.50 = (f32[256,256]{1,0:T(8,128)S(1)}, f32[256,256]{1,0:T(8,128)S(1)}, u32[]{:S(2)}, u32[]{:S(2)}) collective-permute-start(f32[256,256]{1,0:T(8,128)S(1)} %bitcast.38), channel_id=1, source_target_pairs={{0,3},{1,2},{2,1},{3,0},{4,7},{5,6},{6,5},{7,4},{8,11},{9,10},{10,... | collective-permute-start | bytes 786440 | tf_op jit(solution)/shard_map/ppermute | solution.py:591
  300.6 6.7 %collective-permute-start.55 = (f32[64,256]{1,0:T(8,128)}, f32[64,256]{1,0:T(8,128)S(1)}, u32[]{:S(2)}, u32[]{:S(2)}) collective-permute-start(f32[64,256]{1,0:T(8,128)} %get-tuple-element.170), channel_id=1, source_target_pairs={{0,2},{1,3},{2,0},{3,1},{4,6},{5,7},{6,4},{7,5},{8,10},{9,11},{10,... | collective-permute-start | bytes 196616 | tf_op jit(solution)/shard_map/ppermute | solution.py:591
  317.8 6.9 %collective-permute-start.62 = (f32[64,256]{1,0:T(8,128)S(1)}, f32[64,256]{1,0:T(8,128)S(1)}, u32[]{:S(2)}, u32[]{:S(2)}) collective-permute-start(f32[64,256]{1,0:T(8,128)S(1)} %add_add_fusion.1), channel_id=1, source_target_pairs={{0,96},{1,97},{2,98},{3,99},{4,100},{5,101},{6,102},{7,103},{8,104... | collective-permute-start | bytes 196616 | tf_op jit(solution)/shard_map/ppermute | solution.py:591
  319.1 29.2 %collective-permute-start.69 = (f32[512,256]{1,0:T(8,128)}, f32[512,256]{1,0:T(8,128)S(1)}, u32[]{:S(2)}, u32[]{:S(2)}) collective-permute-start(f32[512,256]{1,0:T(8,128)} %get-tuple-element.174.refs_4_), channel_id=1, source_target_pairs={{0,3},{1,2},{2,1},{3,0},{4,7},{5,6},{6,5},{7,4},{8,11},{9,10},{10,... | collective-permute-start | bytes 1572872 | tf_op jit(solution)/shard_map/ppermute | solution.py:591
  320.3 28.0 %collective-permute-start.68 = (f32[512,256]{1,0:T(8,128)}, f32[512,256]{1,0:T(8,128)S(1)}, u32[]{:S(2)}, u32[]{:S(2)}) collective-permute-start(f32[512,256]{1,0:T(8,128)} %get-tuple-element.174.refs_4_), channel_id=1, source_target_pairs={{0,2},{1,3},{2,0},{3,1},{4,6},{5,7},{6,4},{7,5},{8,10},{9,11},{10,... | collective-permute-start | bytes 1572872 | tf_op jit(solution)/shard_map/ppermute | solution.py:591
  320.3 28.0 %collective-permute-start.67 = (f32[512,256]{1,0:T(8,128)}, f32[512,256]{1,0:T(8,128)S(1)}, u32[]{:S(2)}, u32[]{:S(2)}) collective-permute-start(f32[512,256]{1,0:T(8,128)} %get-tuple-element.174.refs_4_), channel_id=1, source_target_pairs={{0,1},{1,0},{2,3},{3,2},{4,5},{5,4},{6,7},{7,6},{8,9},{9,8},{10,11... | collective-permute-start | bytes 1572872 | tf_op jit(solution)/shard_map/ppermute | solution.py:591
  330.4 13.7 %collective-permute-start.66 = (f32[64,256]{1,0:T(8,128)S(1)}, f32[64,256]{1,0:T(8,128)S(1)}, u32[]{:S(2)}, u32[]{:S(2)}) collective-permute-start(f32[64,256]{1,0:T(8,128)S(1)} %add.142.refs_0_), channel_id=1, source_target_pairs={{0,3},{1,2},{2,1},{3,0},{4,7},{5,6},{6,5},{7,4},{8,11},{9,10},{10,... | collective-permute-start | bytes 196616 | tf_op jit(solution)/shard_map/ppermute | solution.py:591
  331.7 13.1 %collective-permute-start.65 = (f32[64,256]{1,0:T(8,128)S(1)}, f32[64,256]{1,0:T(8,128)S(1)}, u32[]{:S(2)}, u32[]{:S(2)}) collective-permute-start(f32[64,256]{1,0:T(8,128)S(1)} %add.142.refs_0_), channel_id=1, source_target_pairs={{0,2},{1,3},{2,0},{3,1},{4,6},{5,7},{6,4},{7,5},{8,10},{9,11},{10,... | collective-permute-start | bytes 196616 | tf_op jit(solution)/shard_map/ppermute | solution.py:591
  (62 other events, 650.5 us)
